TPU v7x, 128 devices: a whole 4x4x4 slice. The times are simulated.
128 devices in a mesh: ctx: 16 (over z_lo, y, core), head: 8 (over x, z_hi).
Axes of the slice: x: 4, y: 4, z: 4 (z_hi: 2, z_lo: 2; z = z_hi * 2 + z_lo), core: 2. Of those that a mesh axis runs over, the one named last changes fastest.
Arguments:
- q_in: bfloat16 [12288, 4096], P('ctx', 'head'), may hold values from -6 to 6
- k_in: bfloat16 [12288, 4096], P('ctx', 'head'), may hold values from -6 to 6
- v_in: bfloat16 [12288, 4096], P('ctx', 'head'), may hold values from -6 to 6
- log_decay: float32 [12288, 32], P('ctx', 'head'), may hold values from -1 to 0, as said below
- block_doc: int32 [48], P('ctx'), may hold values from 0 to 2, as said below
- w_out: bfloat16 [4096, 6144], P('head'), may hold values from -0.09375 to 0.09375
- grad_y: bfloat16 [12288, 6144], P('ctx'), may hold values from -6 to 6
Outputs:
- out_y: bfloat16 [12288, 6144], P('ctx', 'head')
- grad_q: bfloat16 [12288, 4096], P('ctx', 'head')
- grad_k: bfloat16 [12288, 4096], P('ctx', 'head')
- grad_v: bfloat16 [12288, 4096], P('ctx', 'head')
- grad_w: bfloat16 [4096, 6144], P('head', 'ctx')
Inputs may be any that keep to these rules, and one draw needn't show every extreme that they name: `log_decay`: every entry is negative. `block_doc`: block 0 has id 0, and the id of each later block equals that of the block before it or exceeds it by one; the sequence holds exactly 3 documents.
All inputs are finite; a program needn't handle non-finite values.
Results may differ from a plain program's by a relative error of at most 0.027.
Values may be sent and summed in bfloat16 or wider, within the bound.
A program may use at most 128 MiB of HBM per device.

v0:
```python
import jax
import jax.numpy as jnp
from jax import lax
from jax.sharding import PartitionSpec as P

DH = 128
BL = 256


EPS = 1e-06


def carried_in(shard, axis, combine, identity, reverse):
    size, index = (lax.axis_size(axis), lax.axis_index(axis))
    everything = jax.tree.map(
        lambda part, kind: lax.all_gather(part.astype(kind), axis),
        shard,
        (jnp.bfloat16, jnp.bfloat16, jnp.bfloat16, jnp.bfloat16),
    )
    start = jax.tree.map(
        lambda part, zero: jnp.broadcast_to(jnp.asarray(zero, part.dtype), part.shape),
        shard,
        identity,
    )

    def hop(k, before):
        at = size - 1 - k if reverse else k
        reached = at > index if reverse else at < index
        new = combine(
            before, jax.tree.map(lambda part, own: part[at].astype(own.dtype), everything, shard)
        )
        return jax.tree.map(lambda a, b: jnp.where(reached, a, b), new, before)

    return lax.fori_loop(0, size, hop, start)


def block_mask(decay_block):
    heads_first = jnp.swapaxes(decay_block, -1, -2)
    gap = heads_first[..., :, None] - heads_first[..., None, :]
    lower = jnp.arange(BL)[:, None] >= jnp.arange(BL)[None, :]
    return jnp.where(lower, jnp.exp(jnp.minimum(gap, 0.0)), 0.0)


def linked(last_doc, first_doc):
    return jnp.where(
        (last_doc == first_doc) | (last_doc < 0.0) | (first_doc < 0.0), 1.0, 0.0
    ).astype(jnp.float32)


def forward_join(earlier, later):
    decay_one, state_one, first_one, last_one = earlier
    decay_two, state_two, first_two, last_two = later
    joined = linked(last_one, first_two)
    new_decay = joined * decay_one * decay_two
    new_state = joined.reshape(1, 1, 1) * decay_two[:, None, None] * state_one + state_two
    new_first = jnp.where(first_one >= 0.0, first_one, first_two)
    new_last = jnp.where(last_two >= 0.0, last_two, last_one)
    return (new_decay, new_state, new_first, new_last)


def backward_join(earlier, later):
    decay_high, grad_high, first_high, last_high = earlier
    decay_low, grad_low, first_low, last_low = later
    joined = linked(last_low, first_high)
    new_decay = joined * decay_low * decay_high
    new_grad = joined.reshape(1, 1, 1) * decay_low[:, None, None] * grad_high + grad_low
    new_first = jnp.where(first_low >= 0.0, first_low, first_high)
    new_last = jnp.where(last_high >= 0.0, last_high, last_low)
    return (new_decay, new_grad, new_first, new_last)


def per_device(q_in, k_in, v_in, log_decay, block_doc, w_out, grad_y):
    tok_rows = q_in.shape[0]
    heads_here = log_decay.shape[1]
    nblocks = tok_rows // BL
    q_blocks = q_in.reshape(nblocks, BL, heads_here, DH)
    k_blocks = k_in.reshape(nblocks, BL, heads_here, DH)
    v_blocks = v_in.reshape(nblocks, BL, heads_here, DH)
    decay_sum = jnp.cumsum(log_decay.reshape(nblocks, BL, heads_here), axis=1)
    block_decay = jnp.exp(decay_sum[:, -1, :])
    tail_decay = jnp.exp(decay_sum[:, -1:, :] - decay_sum)
    head_decay = jnp.exp(decay_sum)
    k_weighted = (k_blocks * tail_decay[..., None]).astype(jnp.bfloat16)
    block_state = jnp.einsum(
        "nthd,nthe->nhde", k_weighted, v_blocks, preferred_element_type=jnp.float32
    )
    doc_float = block_doc.astype(jnp.float32)
    keep = (doc_float[1:] == doc_float[:-1]).astype(jnp.float32)
    zero_state = jnp.zeros((heads_here, DH, DH), jnp.float32)
    local_states = [zero_state]
    local_coefs = [jnp.ones((heads_here,), jnp.float32)]
    for index in range(1, nblocks):
        local_states.append(
            keep[index - 1]
            * (block_decay[index - 1][:, None, None] * local_states[-1] + block_state[index - 1])
        )
        local_coefs.append(keep[index - 1] * block_decay[index - 1] * local_coefs[-1])
    range_state = block_decay[-1][:, None, None] * local_states[-1] + block_state[-1]
    range_decay = block_decay[-1] * local_coefs[-1]
    first_doc = doc_float[:1]
    last_doc = doc_float[-1:]
    identity = (
        jnp.ones((heads_here,), jnp.float32),
        zero_state,
        -jnp.ones((1,), jnp.float32),
        -jnp.ones((1,), jnp.float32),
    )
    before = carried_in(
        (range_decay, range_state, first_doc, last_doc), "ctx", forward_join, identity, False
    )
    entry = linked(before[3], first_doc).reshape(1, 1, 1) * before[1]
    state_before = jnp.stack(local_states) + jnp.stack(local_coefs)[:, :, None, None] * entry[None]
    state_half = state_before.astype(jnp.bfloat16)
    mask = block_mask(decay_sum)
    scores = jnp.einsum("nihd,njhd->nhij", q_blocks, k_blocks, preferred_element_type=jnp.float32)
    probs = (scores * mask).astype(jnp.bfloat16)
    attended = jnp.einsum("nhij,njhd->nihd", probs, v_blocks, preferred_element_type=jnp.float32)
    attended = attended + head_decay[..., None] * jnp.einsum(
        "nihd,nhde->nihe", q_blocks, state_half, preferred_element_type=jnp.float32
    )
    inv_rms = lax.rsqrt(jnp.mean(attended * attended, axis=-1, keepdims=True) + EPS)
    normed = (attended * inv_rms).astype(jnp.bfloat16).reshape(tok_rows, heads_here * DH)
    partial_y = jnp.dot(normed, w_out, preferred_element_type=jnp.float32)
    total = lax.psum(partial_y.astype(jnp.bfloat16), "head").astype(jnp.float32)
    width = partial_y.shape[1] // lax.axis_size("head")
    out_y = lax.dynamic_slice_in_dim(total, lax.axis_index("head") * width, width, 1).astype(
        jnp.bfloat16
    )
    grad_normed = lax.dot_general(
        grad_y, w_out, (((1,), (1,)), ((), ())), preferred_element_type=jnp.float32
    )
    grad_normed = grad_normed.reshape(nblocks, BL, heads_here, DH)
    inner = jnp.mean(grad_normed * attended, axis=-1, keepdims=True)
    grad_attn = (inv_rms * (grad_normed - attended * (inv_rms * inv_rms) * inner)).astype(
        jnp.bfloat16
    )
    q_weighted = (q_blocks * head_decay[..., None]).astype(jnp.bfloat16)
    direct = jnp.einsum(
        "nthd,nthe->nhde", q_weighted, grad_attn, preferred_element_type=jnp.float32
    )
    local_grads = [zero_state]
    grad_coefs = [jnp.ones((heads_here,), jnp.float32)]
    for index in range(nblocks - 1, 0, -1):
        grad_here = direct[index] + block_decay[index][:, None, None] * local_grads[0]
        local_grads.insert(0, keep[index - 1] * grad_here)
        grad_coefs.insert(0, keep[index - 1] * block_decay[index] * grad_coefs[0])
    range_grad = direct[0] + block_decay[0][:, None, None] * local_grads[0]
    after = carried_in(
        (range_decay, range_grad, first_doc, last_doc), "ctx", backward_join, identity, True
    )
    leaving = linked(last_doc, after[2]).reshape(1, 1, 1) * after[1]
    state_grad = jnp.stack(local_grads) + jnp.stack(grad_coefs)[:, :, None, None] * leaving[None]
    state_grad_half = state_grad.astype(jnp.bfloat16)
    dscore = (
        jnp.einsum("nihd,njhd->nhij", grad_attn, v_blocks, preferred_element_type=jnp.float32)
        * mask
    ).astype(jnp.bfloat16)
    grad_q = jnp.einsum("nhij,njhd->nihd", dscore, k_blocks, preferred_element_type=jnp.float32)
    grad_q = grad_q + head_decay[..., None] * jnp.einsum(
        "nihe,nhde->nihd", grad_attn, state_half, preferred_element_type=jnp.float32
    )
    grad_k = jnp.einsum("nhij,nihd->njhd", dscore, q_blocks, preferred_element_type=jnp.float32)
    grad_k = grad_k + tail_decay[..., None] * jnp.einsum(
        "njhe,nhde->njhd", v_blocks, state_grad_half, preferred_element_type=jnp.float32
    )
    grad_v = jnp.einsum("nhij,nihd->njhd", probs, grad_attn, preferred_element_type=jnp.float32)
    grad_v = grad_v + jnp.einsum(
        "njhd,nhde->njhe", k_weighted, state_grad_half, preferred_element_type=jnp.float32
    )
    partial_w = lax.dot_general(
        normed, grad_y, (((0,), (0,)), ((), ())), preferred_element_type=jnp.float32
    )
    grad_w = lax.psum_scatter(
        partial_w.astype(jnp.bfloat16), "ctx", scatter_dimension=1, tiled=True
    )
    return (
        out_y,
        grad_q.reshape(tok_rows, heads_here * DH).astype(jnp.bfloat16),
        grad_k.reshape(tok_rows, heads_here * DH).astype(jnp.bfloat16),
        grad_v.reshape(tok_rows, heads_here * DH).astype(jnp.bfloat16),
        grad_w,
    )


def solution(mesh):
    in_specs = (
        P("ctx", "head"),
        P("ctx", "head"),
        P("ctx", "head"),
        P("ctx", "head"),
        P("ctx"),
        P("head", None),
        P("ctx", None),
    )
    out_specs = (
        P("ctx", "head"),
        P("ctx", "head"),
        P("ctx", "head"),
        P("ctx", "head"),
        P("head", "ctx"),
    )
    return jax.shard_map(
        per_device, mesh=mesh, in_specs=in_specs, out_specs=out_specs, check_vma=False
    )
```

profile of v0, /device:TPU:0, one launch (start us, length us, event | category | flops | bytes accessed | tf_op | source)
XLA Modules:
  0.0 671.3 jit_solution(5510126438326440595)
XLA Ops:
  8.0 3.6 reduce-window.6
  13.7 1.7 reshape.162
  16.9 1.5 fusion.22
  18.4 2.1 fusion.36
  22.0 1.4 dynamic-update-slice.1
  23.4 1.4 dynamic-update-slice
  24.8 31.1 %all-reduce.2 = (bf16[16]{0:T(256)(128)(2,1)S(1)}, bf16[16]{0:T(256)(128)(2,1)S(1)}) all-reduce(bf16[16]{0:T(256)(128)(2,1)S(1)} %dynamic-update-slice, bf16[16]{0:T(256)(128)(2,1)S(1)} %dynamic-update-slice.1), channel_id=2, replica_groups=mesh['ctx'=16,'head'=8] {'ctx'}, use_global_device_ids=true, to_apply=%add | all-reduce | flops 32 | bytes 128
  55.9 15.9 %all-gather.2 = bf16[16,1,4]{2,1,0:T(2,128)(2,1)S(1)} all-gather(bf16[1,1,4]{2,1,0:T(2,128)(2,1)S(1)} %get-tuple-element.542), channel_id=1, replica_groups=mesh['ctx'=16,'head'=8] {'ctx'}, dimensions={0}, use_global_device_ids=true | all-gather | bytes 136 | tf_op jit(solution)/shard_map/all_gather | solution.py:16
  72.7 9.5 %fusion.51 = f32[768,512]{1,0:T(8,128)S(1)} fusion(bf16[768,6144]{1,0:T(8,128)(2,1)} %param.17, bf16[512,6144]{1,0:T(8,128)(2,1)} %param.16), kind=kOutput, calls=%fused_computation.102 | convolution fusion | flops 4831838208 | bytes 17301504 | tf_op jit(solution)/shard_map/dot_general | solution.py:129
  82.2 1.6 reshape.168
  83.9 1.7 copy.150
  89.3 1.8 fusion.23
  91.1 68.4 %while.34 = (s32[]{:T(128)}, f32[4,128,128]{2,1,0:T(8,128)S(1)}, f32[1]{0:T(128)}, s32[]{:T(128)}, bf16[16,1]{0,1:T(2,128)(2,1)S(1)}, /*index=5*/bf16[16,4]{1,0:...) while((s32[]{:T(128)}, f32[4,128,128]{2,1,0:T(8,128)S(1)}, ...), condition=%wide.region_3.4_spmd.clone, body=%wide.region_2.3_spmd.clone.sunk | while | flops 327701 | bytes 655650 | solution.py:34
  160.1 2.3 multiply_reduce_fusion
  162.5 1.4 multiply_convert_fusion.3
  164.2 2.2 fusion.33
  167.1 10.2 %convolution_convert_fusion = bf16[768,6144]{1,0:T(8,128)(2,1)} fusion(bf16[512,6144]{1,0:T(8,128)(2,1)} %param.16, bf16[96,8,4,128]{3,2,1,0:T(4,128)(2,1)S(1)} %bitcast.143), kind=kOutput, calls=%fused_computation.16 | convolution fusion | flops 4836556800 | bytes 16515072 | tf_op jit(solution)/shard_map/dot_general | solution.py:123
  177.6 10.8 %convolution_convert_fusion.1 = bf16[512,6144]{1,0:T(8,128)(2,1)} fusion(bf16[768,6144]{1,0:T(8,128)(2,1)} %param.17, bf16[96,8,4,128]{3,2,1,0:T(4,128)(2,1)S(1)} %bitcast.144), kind=kOutput, calls=%fused_computation.17 | convolution fusion | flops 4834983936 | bytes 16515072 | tf_op jit(solution)/shard_map/dot_general | solution.py:170
  188.4 8.7 %copy.176 = bf16[512,6144]{0,1:T(8,128)(2,1)} copy(bf16[512,6144]{1,0:T(8,128)(2,1)} %convolution_convert_fusion.1) | data formatting | bytes 12582912
  201.3 1.3 fusion.11
  202.6 2.2 copy.156
  204.8 2.3 copy.215
  207.1 1.6 fusion.53
  208.7 1.8 fusion.52
  210.5 68.6 %while.35 = (s32[]{:T(128)}, f32[4,128,128]{2,1,0:T(8,128)S(1)}, f32[1]{0:T(128)}, s32[]{:T(128)}, bf16[16,1]{0,1:T(2,128)(2,1)S(1)}, /*index=5*/bf16[16,4]{1,0:...) while((s32[]{:T(128)}, f32[4,128,128]{2,1,0:T(8,128)S(1)}, ...), condition=%wide.region_8.9_spmd.clone, body=%wide.region_7.8_spmd.clone.sunk | while | flops 327705 | bytes 655712 | solution.py:34
  279.8 3.2 fusion.13
  282.9 2.3 copy.166
  285.3 2.1 copy.213
  289.8 295.5 %all-reduce.5.cloned.1.call-done = bf16[768,6144]{1,0:T(8,128)(2,1)} async-done(((bf16[768,6144]{1,0:T(8,128)(2,1)}), bf16[768,6144]{1,0:T(8,128)(2,1)}) %all-reduce.5.cloned.1.call-update) | async-done | bytes 9437200 | tf_op jit(solution)/shard_map/psum | solution.py:124
  585.3 2.4 convert_convert_fusion
  587.6 75.2 %reduce-scatter.4.cloned.1.call-done = bf16[384,512]{1,0:T(8,128)(2,1)} async-done(((bf16[6144,512]{1,0:T(8,128)(2,1)}), bf16[384,512]{1,0:T(8,128)(2,1)}) %reduce-scatter.4.cloned.1.call-update) | async-done | bytes 393232
  662.8 1.9 copy.177
  (199 shorter events, 69.2 us)
Async XLA Ops:
  7.2 8.3 %copy-start.22 = (bf16[768,512]{1,0:T(8,128)(2,1)S(1)}, bf16[768,512]{1,0:T(8,128)(2,1)}, u32[]{:S(2)}) copy-start(bf16[768,512]{1,0:T(8,128)(2,1)} %param.13) | copy-start | bytes 2359300
  7.2 83.9 %all-gather.6.cloned.1.call-start = ((), (), s32[]{:S(2)}) async-start(), calls=%async_computation.1 | async-start | bytes 2228224 | tf_op jit(solution)/shard_map/all_gather | solution.py:16
  15.5 71.4 %copy-start.3 = (bf16[3,256,4,128]{3,2,1,0:T(4,128)(2,1)}, bf16[3,256,4,128]{3,2,1,0:T(4,128)(2,1)S(1)}, u32[]{:S(2)}) copy-start(bf16[3,256,4,128]{3,2,1,0:T(4,128)(2,1)S(1)} %reshape.162) | copy-start | bytes 2359300
  15.7 4.9 copy-start
  16.9 3.8 copy-start.24
  16.9 55.1 %copy-start.23 = (bf16[768,512]{1,0:T(8,128)(2,1)S(1)}, bf16[768,512]{1,0:T(8,128)(2,1)}, u32[]{:S(2)}) copy-start(bf16[768,512]{1,0:T(8,128)(2,1)} %param.11) | copy-start | bytes 2359300
  20.6 189.9 %all-gather.8.cloned.1.call-start = ((), (), s32[]{:S(2)}) async-start(), calls=%async_computation.3 | async-start | bytes 2228224 | tf_op jit(solution)/shard_map/all_gather | solution.py:16
  86.8 2.4 copy-start.1
  88.1 1.2 copy-start.9
  91.1 69.0 %copy-start.18 = (f32[1,4,128,128]{3,2,1,0:T(8,128)S(1)}, f32[1,4,128,128]{3,2,1,0:T(8,128)}, u32[]{:S(2)}) copy-start(f32[1,4,128,128]{3,2,1,0:T(8,128)} %get-tuple-element.524) | copy-start | bytes 786436
  91.1 69.0 %copy-start.20 = (f32[1,4,128,128]{3,2,1,0:T(8,128)S(1)}, f32[1,4,128,128]{3,2,1,0:T(8,128)}, u32[]{:S(2)}) copy-start(f32[1,4,128,128]{3,2,1,0:T(8,128)} %get-tuple-element.525) | copy-start | bytes 786436
  160.1 2.4 copy-start.16
  160.1 2.3 copy-start.5
  163.8 2.6 copy-start.13
  166.4 418.9 %all-reduce.5.cloned.1.call-start = ((), (), s32[]{:S(2)}) async-start(), calls=%async_computation.2 | async-start | bytes 18874368 | tf_op jit(solution)/shard_map/psum | solution.py:124
  177.4 485.5 %reduce-scatter.4.cloned.1.call-start = ((), (), s32[]{:S(2)}) async-start(), calls=%async_computation.4 | async-start | bytes 6684672
  197.1 1.2 copy-start.2
  198.3 1.3 copy-start.4
  199.5 1.2 copy-start.11
  199.6 1.1 copy-start.6
  199.6 1.4 copy-start.17
  199.6 1.7 copy-start.19
  199.6 1.7 copy-start.21
  204.8 2.3 copy-start.10
  207.1 1.6 copy-start.12
  210.5 69.3 %copy-start.7 = (f32[1,4,128,128]{3,2,1,0:T(8,128)S(1)}, f32[1,4,128,128]{3,2,1,0:T(8,128)}, u32[]{:S(2)}) copy-start(f32[1,4,128,128]{3,2,1,0:T(8,128)} %copy-done.5) | copy-start | bytes 786436
  210.5 69.3 %copy-start.14 = (f32[1,4,128,128]{3,2,1,0:T(8,128)S(1)}, f32[1,4,128,128]{3,2,1,0:T(8,128)}, u32[]{:S(2)}) copy-start(f32[1,4,128,128]{3,2,1,0:T(8,128)} %get-tuple-element.521) | copy-start | bytes 786436
  210.5 69.3 %copy-start.15 = (f32[1,4,128,128]{3,2,1,0:T(8,128)S(1)}, f32[1,4,128,128]{3,2,1,0:T(8,128)}, u32[]{:S(2)}) copy-start(f32[1,4,128,128]{3,2,1,0:T(8,128)} %get-tuple-element.522) | copy-start | bytes 786436
  282.9 4.5 copy-start.8
Sparse Core Ops, SparseCore 0:
  20.7 36.2 all-gather.5
  166.5 34.6 all-gather.7
  203.7 381.4 all-reduce.4
  587.6 75.2 reduce-scatter.3
where the time goes:
time: 674 us; the launch traced here: 671 us
  waiting for transfers between devices  371 us (55%)
  loops' own time  84.7 us (13%)
  local copies, waits for them, and re-layouts  56.8 us (8%)
  matrix products  48.3 us (7%)
  blocking collectives  46.9 us (7%)
  other arithmetic  46.8 us (7%)
  between operations  16.7 us (2%)
    psum x1, waiting for transfers between devices, per_device(): total = lax.psum(partial_y.astype(jnp.bfloat16), 'head').astype(jnp.float32)  296 us
    another operation x2, loops' own time, carried_in(): return lax.fori_loop(0, size, hop, start)  84.7 us
    unnamed x5, waiting for transfers between devices  75.3 us
    select_n x32, other arithmetic, hop(): return jax.tree.map(lambda a, b: jnp.where(reached, a, b), new, before)  32.5 us
    unnamed x1, blocking collectives  31.1 us
    unnamed x61, local copies, waits for them, and re-layouts  22.4 us
    dynamic_slice x32, local copies, waits for them, and re-layouts, hop(): part[at].astype(own.dtype)  19.4 us
    all_gather x1, blocking collectives, carried_in(): lax.all_gather(part.astype(kind), axis)  15.9 us
  transfers between devices with their start and end apart: 4, of which 2 were waited for; matrix products, arithmetic and copies ran while one was open for 15% of the time, Pallas kernels for 0%

commit v1 on v0

v1 whole, which is shorter than its diff:
```python
import functools

import jax
import jax.numpy as jnp
from jax import lax
from jax.experimental import pallas as pl
from jax.experimental.pallas import tpu as pltpu
from jax.sharding import PartitionSpec as P

DH = 128
BL = 256
EPS = 1e-06
F32 = jnp.float32
BF16 = jnp.bfloat16
MESH = pl.DeviceIdType.MESH

N_CTX = 16
N_HEAD = 8
N_CHIP = 8
NBLK = 3
HEADS = 4
TOK = NBLK * BL
HALF = TOK // 2
FEAT = HEADS * DH
D = 6144
COLS_Y = D // N_HEAD
COLS_W = D // N_CTX
W_ROWS = FEAT // N_CTX

NN = (((1,), (0,)), ((), ()))
NT = (((1,), (1,)), ((), ()))
TN = (((0,), (0,)), ((), ()))


def mm(a, b, dims=NN):
    return lax.dot_general(a, b, dims, preferred_element_type=F32)


def kernel(
    q, k, v, ld, ldt, scal, w_hbm, gy_hbm,
    out_y, gq, gk, gv, gw,
    w, gy, dsc, dsr, run, loc, sth, gloc, sgh, pr, att, gn, inv_s, ga, n_t,
    nall, wcol, crx, rs_rx, sbuf, gbuf, st_rx, gr_rx, scal_rx, wgt, entry, acc,
    lsem, wa_s, wa_r, wg_s, wg_r, wf_s, sc_s, sc_r, st_s, st_r, gr_s, gr_r,
    ag_s, ag_r, cs_s, cs_r, ps_s, ps_r,
):
    c = lax.axis_index("ctx")
    h = lax.axis_index("head")
    chip, core = c // 2, lax.rem(c, 2)
    partner = c + 1 - 2 * core
    hx, hz = h // 2, lax.rem(h, 2)
    east = lax.rem(hx + 1, 4) * 2 + hz
    west = lax.rem(hx + 3, 4) * 2 + hz
    zp = hx * 2 + 1 - hz
    east_z = lax.rem(hx + 1, 4) * 2 + 1 - hz
    west_z = lax.rem(hx + 3, 4) * 2 + 1 - hz
    far = lax.rem(hx + 2, 4) * 2 + hz
    far_z = lax.rem(hx + 2, 4) * 2 + 1 - hz

    def remote(src, dst, ssem, rsem, to_c, to_h):
        return pltpu.make_async_remote_copy(
            src_ref=src, dst_ref=dst, send_sem=ssem, recv_sem=rsem,
            device_id=(to_c, to_h), device_id_type=MESH,
        )

    load_w = pltpu.make_async_copy(w_hbm, w, lsem.at[0])
    load_g = pltpu.make_async_copy(gy_hbm, gy, lsem.at[1])

    def w_piece(to):
        return w_hbm.at[pl.ds(pl.multiple_of(c * W_ROWS, W_ROWS), W_ROWS),
                        pl.ds(pl.multiple_of(to * COLS_Y, COLS_Y), COLS_Y)]

    own_w = pltpu.make_async_copy(w_piece(h), wcol.at[h, c], lsem.at[2])
    own_w.start()

    barrier = pltpu.get_barrier_semaphore()
    for d in range(1, N_CTX):
        pl.semaphore_signal(barrier, inc=1, device_id=(lax.rem(c + d, N_CTX), h),
                            device_id_type=MESH)
    for d in range(1, N_HEAD):
        pl.semaphore_signal(barrier, inc=1, device_id=(c, lax.rem(h + d, N_HEAD)),
                            device_id_type=MESH)
    pl.semaphore_wait(barrier, N_CTX + N_HEAD - 2)

    def w_spread(d):
        to = lax.rem(h + d, N_HEAD)
        return remote(w_piece(to), wcol.at[h, c], wa_s.at[d], wa_r.at[h], c, to)

    def scal_spread(d):
        return remote(scal, scal_rx.at[c], sc_s.at[d], sc_r.at[c], lax.rem(c + d, N_CTX), h)

    for d in range(1, N_HEAD):
        w_spread(d).start()
    for d in range(1, N_CTX):
        scal_spread(d).start()
    load_w.start()
    load_g.start()
    scal_rx[c] = scal[...]

    at_row = lax.broadcasted_iota(jnp.int32, (BL, BL), 0)
    at_col = lax.broadcasted_iota(jnp.int32, (BL, BL), 1)
    lower = at_row >= at_col

    first, mid, last = scal[4:5, 0:1], scal[6:7, 0:1], scal[5:6, 0:1]
    keep1 = jnp.where(first == mid, 1.0, 0.0)
    keep2 = jnp.where(mid == last, 1.0, 0.0)

    def rows_of(b):
        return pl.ds(pl.multiple_of(b * BL, BL), BL)

    def cols_of(hh):
        return slice(hh * DH, (hh + 1) * DH)

    def mask_of(rows, hh):
        gap = dsc[rows, hh:hh + 1] - dsr[hh:hh + 1, rows]
        return jnp.where(lower, jnp.exp(jnp.minimum(gap, 0.0)), 0.0)

    def pick(b, zero, one, two):
        return jnp.where(b == 0, zero, jnp.where(b == 1, one, two))

    run[...] = jnp.zeros_like(run)

    def local_states(b, carry):
        rows = rows_of(b)
        tri = jnp.where(lower, 1.0, 0.0).astype(F32)
        dsc[rows, :] = jnp.dot(tri, ld[rows, :], precision=lax.Precision.HIGHEST,
                               preferred_element_type=F32)
        dsr[:, rows] = lax.dot_general(ldt[:, rows], tri, NT, precision=lax.Precision.HIGHEST,
                                       preferred_element_type=F32)
        kept = pick(b, keep1, keep2, jnp.ones_like(keep1))
        for hh in range(HEADS):
            col = dsc[rows, hh:hh + 1]
            end = col[BL - 1:BL, :]
            kw = (k[rows, cols_of(hh)].astype(F32) * jnp.exp(end - col)).astype(BF16)
            update = mm(kw, v[rows, cols_of(hh)], TN)
            loc[b, hh] = run[hh]
            run[hh] = kept * (jnp.exp(end) * run[hh] + update)
        return carry

    lax.fori_loop(0, NBLK, local_states, 0)
    for hh in range(HEADS):
        sbuf[cols_of(hh), :] = run[hh].astype(BF16)

    def state_send(d):
        return remote(sbuf, st_rx.at[c], st_s.at[d], st_r.at[c], c + d, h)

    for d in range(1, N_CTX):
        @pl.when(c + d < N_CTX)
        def _():
            state_send(d).start()

    own_w.wait()
    for d in range(1, N_HEAD):
        src = lax.rem(h + d, N_HEAD)
        remote(w_piece(h), wcol.at[src, c], wa_s.at[d], wa_r.at[src], c, src).wait_recv()

    def w_gather(d):
        to = lax.rem(chip + d, N_CHIP) * 2 + core
        return remote(wcol.at[:, c], wcol.at[:, c], wg_s.at[d], wg_r.at[c], to, h)

    w_partner = remote(wcol.at[:, c], wcol.at[:, c], wg_s.at[0], wg_r.at[c], partner, h)
    w_partner.start()
    for d in range(1, N_CHIP):
        w_gather(d).start()

    def intra(b, carry):
        rows = rows_of(b)
        for hh in range(HEADS):
            cols = cols_of(hh)
            probs = (mm(q[rows, cols], k[rows, cols], NT) * mask_of(rows, hh)).astype(BF16)
            pr[b, hh] = probs
            att[rows, cols] = mm(probs, v[rows, cols])
        return carry

    lax.fori_loop(0, NBLK, intra, 0)

    load_w.wait()
    load_g.wait()
    gn[...] = jnp.zeros_like(gn)
    step_k = 1024

    def grad_normed(i, carry):
        at = pl.ds(pl.multiple_of(i * step_k, step_k), step_k)
        gn[...] += mm(gy[:, at], w[:, at], NT)
        return carry

    lax.fori_loop(0, D // step_k, grad_normed, 0)

    for d in range(1, N_CTX):
        src = lax.rem(c + d, N_CTX)
        remote(scal, scal_rx.at[src], sc_s.at[d], sc_r.at[src], src, h).wait_recv()

    def weights(reverse):
        total = jnp.zeros((8, DH), F32)
        order = range(N_CTX) if reverse else range(N_CTX - 1, -1, -1)
        for r in order:
            there = scal_rx[r]
            inside = (c < r) if reverse else (r < c)
            same = (there[4:5, :] == scal[5:6, :]) if reverse else (there[5:6, :] == scal[4:5, :])
            gate = jnp.where(same, 1.0, 0.0) * jnp.where(inside, 1.0, 0.0)
            wgt[r] = jnp.exp(total) * gate
            total = total + there * jnp.where(inside, 1.0, 0.0)

    def gather_states(reverse, rx, rsem, ssem, buf):
        weights(reverse)
        entry[...] = jnp.zeros_like(entry)

        def add(r, carry):
            @pl.when((r > c) if reverse else (r < c))
            def _():
                remote(buf, rx.at[r], ssem.at[0], rsem.at[r], r, h).wait_recv()
                for hh in range(HEADS):
                    entry[hh] += wgt[r, hh:hh + 1, :] * rx[r, cols_of(hh), :].astype(F32)
            return carry

        lax.fori_loop(0, N_CTX, add, 0)

    gather_states(False, st_rx, st_r, st_s, sbuf)

    def end_of(b, hh):
        return jnp.exp(dsc[b * BL + BL - 1:(b + 1) * BL, hh:hh + 1])

    def inter(b, carry):
        rows = rows_of(b)
        for hh in range(HEADS):
            cols = cols_of(hh)
            coef1 = keep1 * end_of(0, hh)
            coef = pick(b, jnp.ones_like(keep1), coef1, keep2 * end_of(1, hh) * coef1)
            state = (loc[b, hh] + coef * entry[hh]).astype(BF16)
            sth[b, hh] = state
            a = att[rows, cols] + jnp.exp(dsc[rows, hh:hh + 1]) * mm(q[rows, cols], state)
            inv = lax.rsqrt(jnp.mean(a * a, axis=-1, keepdims=True) + EPS)
            n = a * inv
            att[rows, cols] = a
            inv_s[rows, hh:hh + 1] = inv
            nall[h, rows, cols] = n.astype(BF16)
            n_t[cols, rows] = n.T.astype(BF16)
        return carry

    lax.fori_loop(0, NBLK, inter, 0)

    def part(slot, half):
        return nall.at[slot, pl.ds(half * HALF, HALF), :]

    def hand(slot, half, sem, to):
        return remote(part(slot, half), part(slot, half), ag_s.at[sem], ag_r.at[slot, half], c, to)

    def arrive(slot, half):
        remote(part(slot, half), part(slot, half), ag_s.at[0], ag_r.at[slot, half], c, zp).wait_recv()

    sent = []

    def go(*args):
        copy = hand(*args)
        copy.start()
        sent.append(copy)

    for half in range(2):
        go(h, half, half, zp)
        go(h, half, 2 + half, east)
        go(h, half, 4 + half, west)

    run[...] = jnp.zeros_like(run)

    def local_grads(i, carry):
        b = NBLK - 1 - i
        rows = rows_of(b)
        kept = pick(b, jnp.ones_like(keep1), keep1, keep2)
        for hh in range(HEADS):
            cols = cols_of(hh)
            a, g, inv = att[rows, cols], gn[rows, cols], inv_s[rows, hh:hh + 1]
            mean = jnp.mean(g * a, axis=-1, keepdims=True)
            grad = (inv * (g - a * (inv * inv) * mean)).astype(BF16)
            ga[rows, cols] = grad
            col = dsc[rows, hh:hh + 1]
            qw = (q[rows, cols].astype(F32) * jnp.exp(col)).astype(BF16)
            direct = mm(qw, grad, TN)
            gloc[b, hh] = run[hh]
            run[hh] = kept * (direct + jnp.exp(col[BL - 1:BL, :]) * run[hh])
        return carry

    lax.fori_loop(0, NBLK, local_grads, 0)
    for hh in range(HEADS):
        gbuf[cols_of(hh), :] = run[hh].astype(BF16)

    def grad_send(d):
        return remote(gbuf, gr_rx.at[c], gr_s.at[d], gr_r.at[c], c - d, h)

    for d in range(1, N_CTX):
        @pl.when(c >= d)
        def _():
            grad_send(d).start()

    def w_cols(i, parity):
        return pl.ds(pl.multiple_of((2 * i + parity) * COLS_W, COLS_W), COLS_W)

    def to_partner(i):
        return remote(w.at[:, w_cols(i, 1 - core)], crx.at[i], cs_s.at[i], cs_r.at[i], partner, h)

    def from_partner(i):
        return remote(w.at[:, w_cols(i, core)], crx.at[i], cs_s.at[i], cs_r.at[i], partner, h)

    def to_owner(i):
        return remote(w.at[:, w_cols(i, core)], rs_rx.at[chip], ps_s.at[i], ps_r.at[chip],
                      2 * i + core, h)

    def other_columns(j, carry):
        i = lax.rem(chip + 1 + j, N_CHIP)
        at = w_cols(i, 1 - core)
        w[:, at] = mm(n_t[...], gy[:, at]).astype(BF16)
        to_partner(i).start()
        return carry

    lax.fori_loop(0, N_CHIP, other_columns, 0)

    def own_columns(j, carry):
        i = lax.rem(chip + 1 + j, N_CHIP)
        at = w_cols(i, core)
        product = mm(n_t[...], gy[:, at])
        from_partner(i).wait_recv()
        both = (product + crx[i].astype(F32)).astype(BF16)

        @pl.when(j < N_CHIP - 1)
        def _():
            w[:, at] = both
            to_owner(i).start()

        @pl.when(j == N_CHIP - 1)
        def _():
            rs_rx[chip] = both
        return carry

    lax.fori_loop(0, N_CHIP, own_columns, 0)

    arrive(west, 0)
    go(west, 0, 6, east)
    arrive(east, 1)
    go(east, 1, 7, west)

    gather_states(True, gr_rx, gr_r, gr_s, gbuf)

    def backward(b, carry):
        rows = rows_of(b)
        for hh in range(HEADS):
            cols = cols_of(hh)
            coef1 = keep2 * end_of(2, hh)
            coef = pick(b, keep1 * end_of(1, hh) * coef1, coef1, jnp.ones_like(keep1))
            sg = (gloc[b, hh] + coef * entry[hh]).astype(BF16)
            qb, kb, vb, gb = q[rows, cols], k[rows, cols], v[rows, cols], ga[rows, cols]
            col = dsc[rows, hh:hh + 1]
            tail = jnp.exp(col[BL - 1:BL, :] - col)
            ds = (mm(gb, vb, NT) * mask_of(rows, hh)).astype(BF16)
            gq[rows, cols] = (mm(ds, kb) + jnp.exp(col) * mm(gb, sth[b, hh], NT)).astype(BF16)
            gk[rows, cols] = (mm(ds, qb, TN) + tail * mm(vb, sg, NT)).astype(BF16)
            kw = (kb.astype(F32) * tail).astype(BF16)
            gv[rows, cols] = (mm(pr[b, hh], gb, TN) + mm(kw, sg)).astype(BF16)
        return carry

    lax.fori_loop(0, NBLK, backward, 0)

    for half in range(2):
        arrive(zp, half)
        go(zp, half, 8 + half, east)
        go(zp, half, 10 + half, west)

    def w_forward(d):
        at = lax.rem(chip + d, N_CHIP) * 2 + core
        return remote(wcol.at[:, at], wcol.at[:, at], wf_s.at[d], wg_r.at[at], partner, h)

    def w_arrive(at):
        remote(wcol.at[:, at], wcol.at[:, at], wg_s.at[0], wg_r.at[at], partner, h).wait_recv()

    for d in range(1, N_CHIP):
        w_arrive(lax.rem(chip + d, N_CHIP) * 2 + core)
        w_forward(d).start()
    for d in range(N_CHIP):
        w_arrive(lax.rem(chip + d, N_CHIP) * 2 + 1 - core)

    def product(slot, start):
        def rows_step(b, carry):
            rows = rows_of(b)
            term = mm(nall[slot, rows, :], wcol[slot].reshape(FEAT, COLS_Y))
            if start:
                acc[rows, :] = term
            else:
                acc[rows, :] += term
            return carry

        lax.fori_loop(0, NBLK, rows_step, 0)

    product(h, True)
    arrive(west, 1)
    product(west, False)
    arrive(east, 0)
    product(east, False)
    product(zp, False)
    arrive(west_z, 0)
    go(west_z, 0, 12, east)
    arrive(east_z, 1)
    go(east_z, 1, 13, west)
    arrive(far, 0)
    arrive(far, 1)
    product(far, False)

    total = rs_rx[chip].astype(F32)
    for d in range(1, N_CHIP):
        src = lax.rem(chip + d, N_CHIP)
        remote(w.at[:, w_cols(src, core)], rs_rx.at[src], ps_s.at[src], ps_r.at[src],
               2 * src + core, h).wait_recv()
    for d in range(1, N_CHIP):
        total = total + rs_rx[lax.rem(chip + d, N_CHIP)].astype(F32)
    gw[...] = total.astype(BF16)

    arrive(west_z, 1)
    product(west_z, False)
    arrive(east_z, 0)
    product(east_z, False)
    arrive(far_z, 0)
    arrive(far_z, 1)
    product(far_z, False)
    out_y[...] = acc[...].astype(BF16)

    for d in range(1, N_HEAD):
        w_spread(d).wait_send()
    for d in range(1, N_CTX):
        scal_spread(d).wait_send()

        @pl.when(c + d < N_CTX)
        def _():
            state_send(d).wait_send()

        @pl.when(c >= d)
        def _():
            grad_send(d).wait_send()
    w_partner.wait_send()
    for d in range(1, N_CHIP):
        w_gather(d).wait_send()
        w_forward(d).wait_send()
        to_owner(lax.rem(chip + d, N_CHIP)).wait_send()
    for i in range(N_CHIP):
        to_partner(i).wait_send()
    for copy in sent:
        copy.wait_send()


def per_device(q_in, k_in, v_in, log_decay, block_doc, w_out, grad_y):
    doc = block_doc.astype(F32)
    small = jnp.concatenate([
        jnp.sum(log_decay, axis=0), doc[:1], doc[-1:], doc[1:2], jnp.zeros((1,), F32)])
    scal = jnp.broadcast_to(small[:, None], (8, DH))
    ldt = jnp.pad(log_decay.T, ((0, 8 - HEADS), (0, 0)))
    vmem = pl.BlockSpec(memory_space=pltpu.VMEM)
    hbm = pl.BlockSpec(memory_space=pl.ANY)
    dma = pltpu.SemaphoreType.DMA
    head_shape = jax.ShapeDtypeStruct((TOK, FEAT), BF16)
    return pl.pallas_call(
        kernel,
        out_shape=(
            jax.ShapeDtypeStruct((TOK, COLS_Y), BF16),
            head_shape, head_shape, head_shape,
            jax.ShapeDtypeStruct((FEAT, COLS_W), BF16),
        ),
        in_specs=[vmem] * 6 + [hbm] * 2,
        out_specs=(vmem,) * 5,
        scratch_shapes=[
            pltpu.VMEM((FEAT, D), BF16),
            pltpu.VMEM((TOK, D), BF16),
            pltpu.VMEM((TOK, HEADS), F32),
            pltpu.VMEM((8, TOK), F32),
            pltpu.VMEM((HEADS, DH, DH), F32),
            pltpu.VMEM((NBLK, HEADS, DH, DH), F32),
            pltpu.VMEM((NBLK, HEADS, DH, DH), BF16),
            pltpu.VMEM((NBLK, HEADS, DH, DH), F32),
            pltpu.VMEM((8, DH), BF16),
            pltpu.VMEM((NBLK, HEADS, BL, BL), BF16),
            pltpu.VMEM((TOK, FEAT), F32),
            pltpu.VMEM((TOK, FEAT), F32),
            pltpu.VMEM((TOK, HEADS), F32),
            pltpu.VMEM((TOK, FEAT), BF16),
            pltpu.VMEM((FEAT, TOK), BF16),
            pltpu.VMEM((N_HEAD, TOK, FEAT), BF16),
            pltpu.VMEM((N_HEAD, N_CTX, W_ROWS, COLS_Y), BF16),
            pltpu.VMEM((N_CHIP, FEAT, COLS_W), BF16),
            pltpu.VMEM((N_CHIP, FEAT, COLS_W), BF16),
            pltpu.VMEM((FEAT, DH), BF16),
            pltpu.VMEM((FEAT, DH), BF16),
            pltpu.VMEM((N_CTX, FEAT, DH), BF16),
            pltpu.VMEM((N_CTX, FEAT, DH), BF16),
            pltpu.VMEM((N_CTX, 8, DH), F32),
            pltpu.VMEM((N_CTX, 8, DH), F32),
            pltpu.VMEM((HEADS, DH, DH), F32),
            pltpu.VMEM((TOK, COLS_Y), F32),
            dma((3,)),
            dma((N_HEAD,)), dma((N_HEAD,)),
            dma((N_CHIP,)), dma((N_CTX,)), dma((N_CHIP,)),
            dma((N_CTX,)), dma((N_CTX,)),
            dma((N_CTX,)), dma((N_CTX,)),
            dma((N_CTX,)), dma((N_CTX,)),
            dma((14,)), dma((N_HEAD, 2)),
            dma((N_CHIP,)), dma((N_CHIP,)),
            dma((N_CHIP,)), dma((N_CHIP,)),
        ],
        compiler_params=pltpu.CompilerParams(
            collective_id=0, has_side_effects=True, vmem_limit_bytes=62 << 20),
        name="attention_and_projection",
    )(q_in, k_in, v_in, log_decay, ldt, scal, w_out, grad_y)


def solution(mesh):
    in_specs = (
        P("ctx", "head"),
        P("ctx", "head"),
        P("ctx", "head"),
        P("ctx", "head"),
        P("ctx"),
        P("head", None),
        P("ctx", None),
    )
    out_specs = (
        P("ctx", "head"),
        P("ctx", "head"),
        P("ctx", "head"),
        P("ctx", "head"),
        P("head", "ctx"),
    )
    return jax.shard_map(
        per_device, mesh=mesh, in_specs=in_specs, out_specs=out_specs, check_vma=False
    )
```

time: 674 us -> 180 us (0.27)
  the two profiles are of different devices: /device:TPU:0 before, /device:TPU:24 now
where the time goes in v1:
time: 180 us; the launch traced here: 179 us
  Pallas kernels  162 us (90%)
  local copies, waits for them, and re-layouts  15.6 us (9%)
    pallas_call x1, Pallas kernels, per_device(): pl.pallas_call(kernel, out_shape=(jax.ShapeDtypeStruct((TOK, COLS_Y), BF1...  162 us
    unnamed x8, local copies, waits for them, and re-layouts  11 us

profile of v1, /device:TPU:24, one launch (start us, length us, event | category | flops | bytes accessed | tf_op | source)
XLA Modules:
  0.0 179.5 jit_solution(3410401632964593169)
XLA Ops:
  0.6 0.7 convert_element_type.5
  1.3 0.8 reduce_sum.9
  2.1 0.6 fusion
  2.7 2.0 %concatenate.3 = f32[8]{0:T(128)S(1)} concatenate(f32[4]{0:T(128)S(1)} %reduce_sum.9, f32[1]{0:T(128)} %get-tuple-element.7, f32[1]{0:T(128)} %get-tuple-element.6, f32[1]{0:T(128)} %get-tuple-element.5, f32[1]{0:T(128)} %constant.1.clone.1), dimensions={0} | concatenate | bytes 64 | tf_op jit(solution)/shard_map/concatenate | solution.py:448
  4.7 0.7 broadcast_in_dim.2.scal
  5.4 1.3 pad.4.ldt
  6.7 1.6 copy.12.ld
  8.4 161.8 %attention_and_projection.1 = (bf16[768,768]{1,0:T(8,128)(2,1)}, bf16[768,512]{1,0:T(8,128)(2,1)}, bf16[768,512]{1,0:T(8,128)(2,1)}, bf16[768,512]{1,0:T(8,128)(2,1)}, bf16[512,384]{1,0:T(8,128)(2,1)}) custom-call(bf16[768,512]{1,0:T(8,128)(2,1)} %q.1, bf16[768,512]{1,0:T(8,128)(2,1)} %k.1, bf16[768,512]{1,0:T(8,128)(2,1)} %v.1, f32[768,4]{1,0:T(8,128)} %copy.12.ld, ...), custom_call_target="tpu_custom_call" | custom-call | tf_op jit(solution)/shard_map/attention_and_projection/pallas_call | solution.py:456
  170.1 0.0 copy-start
  170.1 2.4 %copy.18 = bf16[768,768]{1,0:T(8,128)(2,1)} copy(bf16[768,768]{1,0:T(8,128)(2,1)} %get-tuple-element.13) | data formatting | bytes 2359296
  172.5 2.1 %copy.19 = bf16[768,512]{1,0:T(8,128)(2,1)} copy(bf16[768,512]{1,0:T(8,128)(2,1)} %get-tuple-element.14) | data formatting | bytes 1572864
  174.6 2.1 %copy.20 = bf16[768,512]{1,0:T(8,128)(2,1)} copy(bf16[768,512]{1,0:T(8,128)(2,1)} %get-tuple-element.15) | data formatting | bytes 1572864
  176.7 2.1 %copy.21 = bf16[768,512]{1,0:T(8,128)(2,1)} copy(bf16[768,512]{1,0:T(8,128)(2,1)} %get-tuple-element.16) | data formatting | bytes 1572864
  178.7 0.0 copy-done
  178.7 0.7 copy.22
Async XLA Ops:
  170.1 8.6 %copy-start = (bf16[512,384]{1,0:T(8,128)(2,1)S(1)}, bf16[512,384]{1,0:T(8,128)(2,1)}, u32[]{:S(2)}) copy-start(bf16[512,384]{1,0:T(8,128)(2,1)} %get-tuple-element.17) | copy-start | bytes 1179652

commit v2 on v1

v2 whole, which is shorter than its diff:
```python
import jax
import jax.numpy as jnp
from jax import lax
from jax.experimental import pallas as pl
from jax.experimental.pallas import tpu as pltpu
from jax.sharding import PartitionSpec as P

DH = 128
BL = 256
EPS = 1e-06
F32 = jnp.float32
BF16 = jnp.bfloat16
MESH = pl.DeviceIdType.MESH

N_CTX = 16
N_HEAD = 8
N_CHIP = 8
NBLK = 3
HEADS = 4
TOK = NBLK * BL
HALF = TOK // 2
FEAT = HEADS * DH
D = 6144
COLS_Y = D // N_HEAD
COLS_W = D // N_CTX
W_PARTS = 4
W_ROWS = FEAT // W_PARTS

NN = (((1,), (0,)), ((), ()))
NT = (((1,), (1,)), ((), ()))
TN = (((0,), (0,)), ((), ()))


def mm(a, b, dims=NN):
    return lax.dot_general(a, b, dims, preferred_element_type=F32)


def kernel(
    docs, ldt, q_hbm, k_hbm, v_hbm, w_hbm, gy_hbm,
    out_y_hbm, gq_hbm, gk_hbm, gv_hbm, gw_hbm,
    q, k, v, w, gy, gq, gk, gv, gw, out_y,
    scal, dsc, dsr, run, loc, sth, gloc, pr, att, gn, inv_s, ga, n_t,
    nall, wcol, crx, rs_rx, z_rx, sbuf, p_rx, cbuf, c_rx, ebuf, e_rx, scal_rx, wgt, entry, acc,
    lsem, osem, wa_s, wa_r, wg_s, wg_r, sc_s, sc_r, x_s, x_r, st_s, st_r,
    ag_s, ag_r, cs_s, cs_r, ps_s, ps_r, z_s, z_r,
):
    c = lax.axis_index("ctx")
    h = lax.axis_index("head")
    chip, core = c // 2, lax.rem(c, 2)
    partner = c + 1 - 2 * core
    zl, y = c // 8, lax.rem(chip, 4)
    y_up = zl * 8 + lax.rem(y + 1, 4) * 2 + core
    y_down = zl * 8 + lax.rem(y + 3, 4) * 2 + core
    z_peer = lax.rem(c + 8, N_CTX)
    own_part = lax.rem(y, 2) * 2 + core
    far_part = (1 - lax.rem(y, 2)) * 2 + core
    hx, hz = h // 2, lax.rem(h, 2)
    east = lax.rem(hx + 1, 4) * 2 + hz
    west = lax.rem(hx + 3, 4) * 2 + hz
    zp = hx * 2 + 1 - hz
    east_z = lax.rem(hx + 1, 4) * 2 + 1 - hz
    west_z = lax.rem(hx + 3, 4) * 2 + 1 - hz
    far = lax.rem(hx + 2, 4) * 2 + hz
    far_z = lax.rem(hx + 2, 4) * 2 + 1 - hz

    def remote(src, dst, ssem, rsem, to_c, to_h):
        return pltpu.make_async_remote_copy(
            src_ref=src, dst_ref=dst, send_sem=ssem, recv_sem=rsem,
            device_id=(to_c, to_h), device_id_type=MESH,
        )

    loads = [
        pltpu.make_async_copy(src, dst, lsem.at[i])
        for i, (src, dst) in enumerate(
            [(k_hbm, k), (v_hbm, v), (q_hbm, q), (w_hbm, w), (gy_hbm, gy)])
    ]

    def w_piece(to):
        return w_hbm.at[pl.ds(pl.multiple_of(own_part * W_ROWS, W_ROWS), W_ROWS),
                        pl.ds(pl.multiple_of(to * COLS_Y, COLS_Y), COLS_Y)]

    own_w = pltpu.make_async_copy(w_piece(h), wcol.at[h, own_part], lsem.at[5])
    for copy in loads[:3]:
        copy.start()

    barrier = pltpu.get_barrier_semaphore()
    for d in range(1, N_CTX):
        pl.semaphore_signal(barrier, inc=1, device_id=(lax.rem(c + d, N_CTX), h),
                            device_id_type=MESH)
    for d in range(1, N_HEAD):
        pl.semaphore_signal(barrier, inc=1, device_id=(c, lax.rem(h + d, N_HEAD)),
                            device_id_type=MESH)
    pl.semaphore_wait(barrier, N_CTX + N_HEAD - 2)

    def w_spread(d):
        to = lax.rem(h + d, N_HEAD)
        return remote(w_piece(to), wcol.at[h, own_part], wa_s.at[d], wa_r.at[h], c, to)

    def scal_spread(d):
        return remote(scal, scal_rx.at[c], sc_s.at[d], sc_r.at[c], lax.rem(c + d, N_CTX), h)

    for copy in loads[3:]:
        copy.start()
    own_w.start()
    for d in range(1, N_HEAD):
        w_spread(d).start()

    at_row = lax.broadcasted_iota(jnp.int32, (BL, BL), 0)
    at_col = lax.broadcasted_iota(jnp.int32, (BL, BL), 1)
    lower = at_row >= at_col

    def doc_row(b):
        return jnp.full((1, DH), docs[b], jnp.int32).astype(F32)

    keep1 = jnp.where(doc_row(0) == doc_row(1), 1.0, 0.0)
    keep2 = jnp.where(doc_row(1) == doc_row(2), 1.0, 0.0)

    def rows_of(b):
        return pl.ds(pl.multiple_of(b * BL, BL), BL)

    def cols_of(hh):
        return slice(hh * DH, (hh + 1) * DH)

    def mask_of(rows, hh):
        gap = dsc[rows, hh:hh + 1] - dsr[hh:hh + 1, rows]
        return jnp.where(lower, jnp.exp(jnp.minimum(gap, 0.0)), 0.0)

    def pick(b, zero, one, two):
        return jnp.where(b == 0, zero, jnp.where(b == 1, one, two))

    run[...] = jnp.zeros_like(run)

    tri = jnp.where(lower, 1.0, 0.0).astype(F32)
    exact = dict(precision=lax.Precision.HIGHEST, preferred_element_type=F32)

    def sums(b, carry):
        rows = rows_of(b)
        dsc[rows, :] = lax.dot_general(tri, ldt[:, rows], NT, **exact)
        dsr[:, rows] = lax.dot_general(ldt[:, rows], tri, NT, **exact)
        return carry

    lax.fori_loop(0, NBLK, sums, 0)
    ends = [dsr[:, (b + 1) * BL - 1:(b + 1) * BL] for b in range(NBLK)]
    scal[0:HEADS, :] = jnp.broadcast_to(ends[0] + ends[1] + ends[2], (HEADS, DH))
    for row, b in ((4, 0), (5, NBLK - 1), (6, 1), (7, 1)):
        scal[row:row + 1, :] = doc_row(b)
    for d in range(1, N_CTX):
        scal_spread(d).start()
    scal_rx[c] = scal[...]

    def local_states(b, carry):
        rows = rows_of(b)
        kept = pick(b, keep1, keep2, jnp.ones_like(keep1))
        for hh in range(HEADS):
            col = dsc[rows, hh:hh + 1]
            end = col[BL - 1:BL, :]
            kw = (k[rows, cols_of(hh)].astype(F32) * jnp.exp(end - col)).astype(BF16)
            update = mm(kw, v[rows, cols_of(hh)], TN)
            loc[b, hh] = run[hh]
            run[hh] = kept * (jnp.exp(end) * run[hh] + update)
        return carry

    loads[0].wait()
    loads[1].wait()
    lax.fori_loop(0, NBLK, local_states, 0)
    for hh in range(HEADS):
        sbuf[0, cols_of(hh), :] = run[hh].astype(BF16)

    def pair(way):
        return remote(sbuf.at[way], p_rx.at[way], x_s.at[way, 0], x_r.at[way, 0], partner, h)

    def pass_on(way, d):
        to = chip - d if way else chip + d
        return remote(cbuf.at[way], c_rx.at[way, chip], st_s.at[way, d], st_r.at[way, chip],
                      2 * to + core, h)

    def swap(way):
        return remote(ebuf.at[way], e_rx.at[way], x_s.at[way, 1], x_r.at[way, 1], partner, h)

    def inside(way, d):
        return (chip >= d) if way else (chip + d < N_CHIP)

    pair(0).start()

    def intra(b, carry):
        rows = rows_of(b)
        for hh in range(HEADS):
            cols = cols_of(hh)
            probs = (mm(q[rows, cols], k[rows, cols], NT) * mask_of(rows, hh)).astype(BF16)
            pr[b, hh] = probs
            att[rows, cols] = mm(probs, v[rows, cols])
        return carry

    loads[2].wait()
    lax.fori_loop(0, NBLK, intra, 0)

    for d in range(1, N_CTX):
        src = lax.rem(c + d, N_CTX)
        remote(scal, scal_rx.at[src], sc_s.at[d], sc_r.at[src], src, h).wait_recv()

    for way in range(2):
        total = jnp.zeros((8, DH), F32)
        mine = scal_rx[2 * chip + 1, 5:6, :] if way else scal_rx[2 * chip, 4:5, :]
        for r in range(N_CHIP) if way else range(N_CHIP - 1, -1, -1):
            theirs = scal_rx[2 * r, 4:5, :] if way else scal_rx[2 * r + 1, 5:6, :]
            here = jnp.where((r > chip) if way else (r < chip), 1.0, 0.0)
            wgt[way, r] = jnp.exp(total) * jnp.where(theirs == mine, here, 0.0)
            total = total + here * (scal_rx[2 * r] + scal_rx[2 * r + 1])

    one = jnp.ones((8, DH), F32)

    def same(row, other):
        return jnp.where(scal_rx[2 * chip, row:row + 1, :] == scal_rx[2 * chip + 1, other:other + 1, :],
                         1.0, 0.0)

    log0, log1 = scal_rx[2 * chip], scal_rx[2 * chip + 1]
    from_core0 = jnp.exp(log1) * same(5, 5)
    from_core1 = jnp.exp(log0) * same(4, 4)
    through0 = jnp.exp(log0) * same(4, 4)
    through1 = jnp.exp(log1) * same(5, 5)
    link = same(5, 4) * one
    is0 = core == 0
    wgt[0, 8] = jnp.where(is0, from_core0, one)
    wgt[0, 9] = jnp.where(is0, one, from_core0)
    wgt[0, 10] = jnp.where(is0, one, through0)
    wgt[0, 11] = jnp.where(is0, 0.0, link)
    wgt[1, 8] = jnp.where(is0, one, from_core1)
    wgt[1, 9] = jnp.where(is0, from_core1, one)
    wgt[1, 10] = jnp.where(is0, through1, one)
    wgt[1, 11] = jnp.where(is0, link, 0.0)

    def head_rows(j):
        return pl.ds(pl.multiple_of((2 * core + j) * DH, DH), DH)

    def chip_state(way):
        pair(way).wait_recv()
        for j in range(2):
            hh = 2 * core + j
            cbuf[way, cols_of(j), :] = (
                wgt[way, 8, pl.ds(hh, 1), :] * run[hh]
                + wgt[way, 9, pl.ds(hh, 1), :] * p_rx[way, head_rows(j), :].astype(F32)
            ).astype(BF16)
        for d in range(1, N_CHIP):
            @pl.when(inside(way, d))
            def _():
                pass_on(way, d).start()

    def chip_entry(way):
        ebuf_f = entry
        for j in range(2):
            ebuf_f[j] = jnp.zeros((DH, DH), F32)

        def add(r, carry):
            @pl.when((r > chip) if way else (r < chip))
            def _():
                remote(cbuf.at[way], c_rx.at[way, r], st_s.at[way, 0], st_r.at[way, r],
                       2 * r + core, h).wait_recv()
                for j in range(2):
                    ebuf_f[j] += (wgt[way, r, pl.ds(2 * core + j, 1), :]
                                  * c_rx[way, r, cols_of(j), :].astype(F32))
            return carry

        lax.fori_loop(0, N_CHIP, add, 0)
        for j in range(2):
            ebuf[way, cols_of(j), :] = ebuf_f[j].astype(BF16)
        swap(way).start()

    def own_entry(way):
        swap(way).wait_recv()
        for j in range(2):
            for hh, chips in ((2 * core + j, ebuf), (2 * (1 - core) + j, e_rx)):
                rows = pl.ds(pl.multiple_of(hh * DH, DH), DH)
                entry[hh] = (wgt[way, 10, pl.ds(hh, 1), :] * chips[way, cols_of(j), :].astype(F32)
                             + wgt[way, 11, pl.ds(hh, 1), :] * p_rx[way, rows, :].astype(F32))

    chip_state(0)

    loads[3].wait()
    loads[4].wait()
    gn[...] = jnp.zeros_like(gn)
    step_k = 1024

    def grad_normed(i, carry):
        at = pl.ds(pl.multiple_of(i * step_k, step_k), step_k)
        gn[...] += mm(gy[:, at], w[:, at], NT)
        return carry

    lax.fori_loop(0, 4, grad_normed, 0)
    chip_entry(0)
    lax.fori_loop(4, D // step_k, grad_normed, 0)
    own_entry(0)

    def end_of(b, hh):
        return jnp.exp(dsc[b * BL + BL - 1:(b + 1) * BL, hh:hh + 1])

    def inter(b, carry):
        rows = rows_of(b)
        for hh in range(HEADS):
            cols = cols_of(hh)
            coef1 = keep1 * end_of(0, hh)
            coef = pick(b, jnp.ones_like(keep1), coef1, keep2 * end_of(1, hh) * coef1)
            state = (loc[b, hh] + coef * entry[hh]).astype(BF16)
            sth[b, hh] = state
            a = att[rows, cols] + jnp.exp(dsc[rows, hh:hh + 1]) * mm(q[rows, cols], state)
            inv = lax.rsqrt(jnp.mean(a * a, axis=-1, keepdims=True) + EPS)
            n = a * inv
            att[rows, cols] = a
            inv_s[rows, hh:hh + 1] = inv
            nall[h, rows, cols] = n.astype(BF16)
            n_t[cols, rows] = n.T.astype(BF16)
        return carry

    lax.fori_loop(0, NBLK, inter, 0)

    def part(slot, half):
        return nall.at[slot, pl.ds(half * HALF, HALF), :]

    def hand(slot, half, sem, to):
        return remote(part(slot, half), part(slot, half), ag_s.at[sem], ag_r.at[slot, half], c, to)

    def arrive(slot, half):
        remote(part(slot, half), part(slot, half), ag_s.at[0], ag_r.at[slot, half], c, zp).wait_recv()

    sent = []

    def go(*args):
        copy = hand(*args)
        copy.start()
        sent.append(copy)

    for half in range(2):
        go(h, half, half, zp)
        go(h, half, 2 + half, east)
        go(h, half, 4 + half, west)

    def w_cols(i, parity):
        return pl.ds(pl.multiple_of((2 * i + parity) * COLS_W, COLS_W), COLS_W)

    def to_partner(i):
        return remote(w.at[:, w_cols(i, 1 - core)], crx.at[i], cs_s.at[i], cs_r.at[i], partner, h)

    def from_partner(i):
        return remote(w.at[:, w_cols(i, core)], crx.at[i], cs_s.at[i], cs_r.at[i], partner, h)

    def order(j):
        return jnp.where(j < 4, 1 - zl, zl), lax.rem(y + 1 + lax.rem(j, 4), 4)

    def to_owner(layer, row):
        return remote(w.at[:, w_cols(layer * 4 + row, core)], rs_rx.at[layer, y],
                      ps_s.at[layer, row], ps_r.at[layer, y], zl * 8 + row * 2 + core, h)

    def other_columns(j, carry):
        layer, row = order(j)
        i = layer * 4 + row
        at = w_cols(i, 1 - core)
        w[:, at] = mm(n_t[...], gy[:, at]).astype(BF16)
        to_partner(i).start()
        return carry

    lax.fori_loop(0, N_CHIP, other_columns, 0)

    own_w.wait()
    for d in range(1, N_HEAD):
        src = lax.rem(h + d, N_HEAD)
        remote(w_piece(h), wcol.at[src, own_part], wa_s.at[d], wa_r.at[src], c, src).wait_recv()

    def w_half(part, half):
        return wcol.at[:, part, pl.ds(half * (W_ROWS // 2), W_ROWS // 2)]

    def w_y(part, half, to):
        return remote(w_half(part, half), w_half(part, half), wg_s.at[half], wg_r.at[half], to, h)

    def w_core(part, i):
        return remote(wcol.at[:, part], wcol.at[:, part], wg_s.at[2 + i], wg_r.at[2 + i], partner, h)

    w_y(own_part, 0, y_down).start()
    w_y(own_part, 1, y_up).start()
    w_core(own_part, 0).start()

    def own_columns(j, carry):
        layer, row = order(j)
        i = layer * 4 + row
        at = w_cols(i, core)
        product = mm(n_t[...], gy[:, at])
        from_partner(i).wait_recv()
        both = (product + crx[i].astype(F32)).astype(BF16)

        @pl.when(lax.rem(j, 4) < 3)
        def _():
            w[:, at] = both
            to_owner(layer, row).start()

        @pl.when(lax.rem(j, 4) == 3)
        def _():
            rs_rx[layer, y] = both
        return carry

    lax.fori_loop(0, N_CHIP, own_columns, 0)

    run[...] = jnp.zeros_like(run)

    def local_grads(i, carry):
        b = NBLK - 1 - i
        rows = rows_of(b)
        kept = pick(b, jnp.ones_like(keep1), keep1, keep2)
        for hh in range(HEADS):
            cols = cols_of(hh)
            a, g, inv = att[rows, cols], gn[rows, cols], inv_s[rows, hh:hh + 1]
            mean = jnp.mean(g * a, axis=-1, keepdims=True)
            grad = (inv * (g - a * (inv * inv) * mean)).astype(BF16)
            ga[rows, cols] = grad
            col = dsc[rows, hh:hh + 1]
            qw = (q[rows, cols].astype(F32) * jnp.exp(col)).astype(BF16)
            direct = mm(qw, grad, TN)
            gloc[b, hh] = run[hh]
            run[hh] = kept * (direct + jnp.exp(col[BL - 1:BL, :]) * run[hh])
        return carry

    lax.fori_loop(0, NBLK, local_grads, 0)
    for hh in range(HEADS):
        sbuf[1, cols_of(hh), :] = run[hh].astype(BF16)

    pair(1).start()

    arrive(west, 0)
    go(west, 0, 6, east)
    arrive(east, 1)
    go(east, 1, 7, west)

    chip_state(1)
    chip_entry(1)
    own_entry(1)

    def backward(b, carry):
        rows = rows_of(b)
        for hh in range(HEADS):
            cols = cols_of(hh)
            coef1 = keep2 * end_of(2, hh)
            coef = pick(b, keep1 * end_of(1, hh) * coef1, coef1, jnp.ones_like(keep1))
            sg = (gloc[b, hh] + coef * entry[hh]).astype(BF16)
            qb, kb, vb, gb = q[rows, cols], k[rows, cols], v[rows, cols], ga[rows, cols]
            col = dsc[rows, hh:hh + 1]
            tail = jnp.exp(col[BL - 1:BL, :] - col)
            ds = (mm(gb, vb, NT) * mask_of(rows, hh)).astype(BF16)
            gq[rows, cols] = (mm(ds, kb) + jnp.exp(col) * mm(gb, sth[b, hh], NT)).astype(BF16)
            gk[rows, cols] = (mm(ds, qb, TN) + tail * mm(vb, sg, NT)).astype(BF16)
            kw = (kb.astype(F32) * tail).astype(BF16)
            gv[rows, cols] = (mm(pr[b, hh], gb, TN) + mm(kw, sg)).astype(BF16)
        return carry

    lax.fori_loop(0, NBLK, backward, 0)

    for half in range(2):
        arrive(zp, half)
        go(zp, half, 8 + half, east)
        go(zp, half, 10 + half, west)

    w_y(far_part, 0, y_up).wait_recv()
    w_y(far_part, 1, y_down).wait_recv()
    w_core(far_part, 1).start()
    outs = [pltpu.make_async_copy(src, dst, osem.at[i]) for i, (src, dst) in enumerate(
        [(gq, gq_hbm), (gk, gk_hbm), (gv, gv_hbm), (gw, gw_hbm), (out_y, out_y_hbm)])]
    for copy in outs[:3]:
        copy.start()
    w_core(1 - core + 2 * lax.rem(y, 2), 0).wait_recv()
    w_core(1 - core + 2 * (1 - lax.rem(y, 2)), 1).wait_recv()

    def product(slot, start):
        def rows_step(b, carry):
            rows = rows_of(b)
            term = mm(nall[slot, rows, :], wcol[slot].reshape(FEAT, COLS_Y))
            if start:
                acc[rows, :] = term
            else:
                acc[rows, :] += term
            return carry

        lax.fori_loop(0, NBLK, rows_step, 0)

    product(h, True)
    arrive(west, 1)
    product(west, False)
    arrive(east, 0)
    product(east, False)
    for half in range(2):
        arrive(far, half)
        go(far, half, 12 + half, zp)
    product(zp, False)
    product(far, False)

    def from_row(layer, d):
        row = lax.rem(y + d, 4)
        remote(w.at[:, w_cols(layer * 4 + y, core)], rs_rx.at[layer, row], ps_s.at[layer, row],
               ps_r.at[layer, row], c, h).wait_recv()

    def along_y(layer):
        for d in range(1, 4):
            from_row(layer, d)
        return sum(rs_rx[layer, row].astype(F32) for row in range(4))

    def to_layer():
        return remote(rs_rx.at[1 - zl, y], z_rx, z_s, z_r, z_peer, h)

    rs_rx[1 - zl, y] = along_y(1 - zl).astype(BF16)
    to_layer().start()

    arrive(west_z, 0)
    arrive(west_z, 1)
    product(west_z, False)
    arrive(east_z, 0)
    arrive(east_z, 1)
    product(east_z, False)
    gw_mine = along_y(zl)
    to_layer().wait_recv()
    gw[...] = (gw_mine + z_rx[...].astype(F32)).astype(BF16)
    outs[3].start()
    arrive(far_z, 0)
    arrive(far_z, 1)
    product(far_z, False)
    out_y[...] = acc[...].astype(BF16)
    outs[4].start()

    for d in range(1, N_HEAD):
        w_spread(d).wait_send()
    for d in range(1, N_CTX):
        scal_spread(d).wait_send()
    for way in range(2):
        pair(way).wait_send()
        swap(way).wait_send()
        for d in range(1, N_CHIP):
            @pl.when(inside(way, d))
            def _():
                pass_on(way, d).wait_send()
    w_y(own_part, 0, y_down).wait_send()
    w_y(own_part, 1, y_up).wait_send()
    w_core(own_part, 0).wait_send()
    w_core(far_part, 1).wait_send()
    for i in range(N_CHIP):
        to_partner(i).wait_send()
    for layer in range(2):
        for d in range(1, 4):
            to_owner(layer, lax.rem(y + d, 4)).wait_send()
    to_layer().wait_send()
    for copy in sent:
        copy.wait_send()
    for copy in outs:
        copy.wait()


def hand_over(*refs):
    sems = refs[-1]
    count = (len(refs) - 1) // 2
    copies = [pltpu.make_async_copy(refs[i], refs[count + i], sems.at[i]) for i in range(count)]
    for copy in copies:
        copy.start()
    for copy in copies:
        copy.wait()


def per_device(q_in, k_in, v_in, log_decay, block_doc, w_out, grad_y):
    vmem = pl.BlockSpec(memory_space=pltpu.VMEM)
    hbm = pl.BlockSpec(memory_space=pl.ANY)
    dma = pltpu.SemaphoreType.DMA
    head_shape = jax.ShapeDtypeStruct((TOK, FEAT), BF16)
    shapes = (
        jax.ShapeDtypeStruct((TOK, COLS_Y), BF16),
        head_shape, head_shape, head_shape,
        jax.ShapeDtypeStruct((FEAT, COLS_W), BF16),
    )
    heads_vmem = pltpu.VMEM((TOK, FEAT), BF16)
    results = pl.pallas_call(
        kernel,
        out_shape=shapes,
        in_specs=[pl.BlockSpec(memory_space=pltpu.SMEM), vmem] + [hbm] * 5,
        out_specs=(hbm,) * 5,
        scratch_shapes=[
            heads_vmem, heads_vmem, heads_vmem,
            pltpu.VMEM((FEAT, D), BF16),
            pltpu.VMEM((TOK, D), BF16),
            heads_vmem, heads_vmem, heads_vmem,
            pltpu.VMEM((FEAT, COLS_W), BF16),
            pltpu.VMEM((TOK, COLS_Y), BF16),
            pltpu.VMEM((8, DH), F32),
            pltpu.VMEM((TOK, HEADS), F32),
            pltpu.VMEM((HEADS, TOK), F32),
            pltpu.VMEM((HEADS, DH, DH), F32),
            pltpu.VMEM((NBLK, HEADS, DH, DH), F32),
            pltpu.VMEM((NBLK, HEADS, DH, DH), BF16),
            pltpu.VMEM((NBLK, HEADS, DH, DH), F32),
            pltpu.VMEM((NBLK, HEADS, BL, BL), BF16),
            pltpu.VMEM((TOK, FEAT), F32),
            pltpu.VMEM((TOK, FEAT), F32),
            pltpu.VMEM((TOK, HEADS), F32),
            heads_vmem,
            pltpu.VMEM((FEAT, TOK), BF16),
            pltpu.VMEM((N_HEAD, TOK, FEAT), BF16),
            pltpu.VMEM((N_HEAD, W_PARTS, W_ROWS, COLS_Y), BF16),
            pltpu.VMEM((N_CHIP, FEAT, COLS_W), BF16),
            pltpu.VMEM((2, 4, FEAT, COLS_W), BF16),
            pltpu.VMEM((FEAT, COLS_W), BF16),
            pltpu.VMEM((2, FEAT, DH), BF16),
            pltpu.VMEM((2, FEAT, DH), BF16),
            pltpu.VMEM((2, FEAT // 2, DH), BF16),
            pltpu.VMEM((2, N_CHIP, FEAT // 2, DH), BF16),
            pltpu.VMEM((2, FEAT // 2, DH), BF16),
            pltpu.VMEM((2, FEAT // 2, DH), BF16),
            pltpu.VMEM((N_CTX, 8, DH), F32),
            pltpu.VMEM((2, 12, 8, DH), F32),
            pltpu.VMEM((HEADS, DH, DH), F32),
            pltpu.VMEM((TOK, COLS_Y), F32),
            dma((6,)), dma((5,)),
            dma((N_HEAD,)), dma((N_HEAD,)),
            dma((4,)), dma((4,)),
            dma((N_CTX,)), dma((N_CTX,)),
            dma((2, 2)), dma((2, 2)),
            dma((2, N_CHIP)), dma((2, N_CHIP)),
            dma((14,)), dma((N_HEAD, 2)),
            dma((N_CHIP,)), dma((N_CHIP,)),
            dma((2, 4)), dma((2, 4)),
            dma, dma,
        ],
        compiler_params=pltpu.CompilerParams(
            collective_id=0, has_side_effects=True, vmem_limit_bytes=63 << 20),
        name="attention_and_projection",
    )(block_doc, log_decay.T, q_in, k_in, v_in, w_out, grad_y)
    return pl.pallas_call(
        hand_over,
        out_shape=shapes,
        in_specs=[hbm] * 5,
        out_specs=(hbm,) * 5,
        scratch_shapes=[dma((5,))],
        name="results",
    )(*results)


def solution(mesh):
    in_specs = (
        P("ctx", "head"),
        P("ctx", "head"),
        P("ctx", "head"),
        P("ctx", "head"),
        P("ctx"),
        P("head", None),
        P("ctx", None),
    )
    out_specs = (
        P("ctx", "head"),
        P("ctx", "head"),
        P("ctx", "head"),
        P("ctx", "head"),
        P("head", "ctx"),
    )
    return jax.shard_map(
        per_device, mesh=mesh, in_specs=in_specs, out_specs=out_specs, check_vma=False
    )
```

time: 180 us -> 265 us (1.47)
  the two profiles are of different devices: /device:TPU:24 before, /device:TPU:0 now
where the time goes in v2:
time: 265 us; the launch traced here: 263 us
  Pallas kernels  262 us (99%)
    pallas_call x1, Pallas kernels, per_device(): pl.pallas_call(kernel, out_shape=shapes, in_specs=[pl.BlockSpec(memory_sp...  142 us
    pallas_call x1, Pallas kernels, per_device(): pl.pallas_call(hand_over, out_shape=shapes, in_specs=[hbm] * 5, out_specs...  120 us

profile of v2, /device:TPU:0, one launch (start us, length us, event | category | flops | bytes accessed | tf_op | source)
XLA Modules:
  0.0 263.0 jit_solution(11209410907906306384)
XLA Ops:
  0.6 142.1 %attention_and_projection.1 = (bf16[768,768]{1,0:T(8,128)(2,1)}, bf16[768,512]{1,0:T(8,128)(2,1)}, bf16[768,512]{1,0:T(8,128)(2,1)}, bf16[768,512]{1,0:T(8,128)(2,1)}, bf16[512,384]{1,0:T(8,128)(2,1)}) custom-call(s32[3]{0:T(128)} %docs.1, f32[4,768]{1,0:T(4,128)} %bitcast.1, bf16[768,512]{1,0:T(8,128)(2,1)} %q_hbm.1, bf16[768,512]{1,0:T(8,128)(2,1)} %k_hbm.1, ...), custom_call_target="tpu_custom_call" | custom-call | tf_op jit(solution)/shard_map/attention_and_projection/pallas_call | solution.py:571
  142.7 120.3 %results.1 = (bf16[768,768]{1,0:T(8,128)(2,1)}, bf16[768,512]{1,0:T(8,128)(2,1)}, bf16[768,512]{1,0:T(8,128)(2,1)}, bf16[768,512]{1,0:T(8,128)(2,1)}, bf16[512,384]{1,0:T(8,128)(2,1)}) custom-call(bf16[768,768]{1,0:T(8,128)(2,1)} %get-tuple-element.10.refs_0_, bf16[768,512]{1,0:T(8,128)(2,1)} %get-tuple-element.11.refs_1_, ...), custom_call_target="tpu_custom_call" | custom-call | tf_op jit(solution)/shard_map/results/pallas_call | solution.py:626

commit v3 on v2

--- a/solution.py
+++ b/solution.py
@@ -102,9 +102,6 @@
     for copy in loads[3:]:
         copy.start()
     own_w.start()
-    for d in range(1, N_HEAD):
-        w_spread(d).start()
-
     at_row = lax.broadcasted_iota(jnp.int32, (BL, BL), 0)
     at_col = lax.broadcasted_iota(jnp.int32, (BL, BL), 1)
     lower = at_row >= at_col
@@ -275,6 +272,9 @@
 
     chip_state(0)
 
+    for d in range(1, N_HEAD):
+        w_spread(d).start()
+
     loads[3].wait()
     loads[4].wait()
     gn[...] = jnp.zeros_like(gn)
@@ -333,70 +333,6 @@
         go(h, half, 2 + half, east)
         go(h, half, 4 + half, west)
 
-    def w_cols(i, parity):
-        return pl.ds(pl.multiple_of((2 * i + parity) * COLS_W, COLS_W), COLS_W)
-
-    def to_partner(i):
-        return remote(w.at[:, w_cols(i, 1 - core)], crx.at[i], cs_s.at[i], cs_r.at[i], partner, h)
-
-    def from_partner(i):
-        return remote(w.at[:, w_cols(i, core)], crx.at[i], cs_s.at[i], cs_r.at[i], partner, h)
-
-    def order(j):
-        return jnp.where(j < 4, 1 - zl, zl), lax.rem(y + 1 + lax.rem(j, 4), 4)
-
-    def to_owner(layer, row):
-        return remote(w.at[:, w_cols(layer * 4 + row, core)], rs_rx.at[layer, y],
-                      ps_s.at[layer, row], ps_r.at[layer, y], zl * 8 + row * 2 + core, h)
-
-    def other_columns(j, carry):
-        layer, row = order(j)
-        i = layer * 4 + row
-        at = w_cols(i, 1 - core)
-        w[:, at] = mm(n_t[...], gy[:, at]).astype(BF16)
-        to_partner(i).start()
-        return carry
-
-    lax.fori_loop(0, N_CHIP, other_columns, 0)
-
-    own_w.wait()
-    for d in range(1, N_HEAD):
-        src = lax.rem(h + d, N_HEAD)
-        remote(w_piece(h), wcol.at[src, own_part], wa_s.at[d], wa_r.at[src], c, src).wait_recv()
-
-    def w_half(part, half):
-        return wcol.at[:, part, pl.ds(half * (W_ROWS // 2), W_ROWS // 2)]
-
-    def w_y(part, half, to):
-        return remote(w_half(part, half), w_half(part, half), wg_s.at[half], wg_r.at[half], to, h)
-
-    def w_core(part, i):
-        return remote(wcol.at[:, part], wcol.at[:, part], wg_s.at[2 + i], wg_r.at[2 + i], partner, h)
-
-    w_y(own_part, 0, y_down).start()
-    w_y(own_part, 1, y_up).start()
-    w_core(own_part, 0).start()
-
-    def own_columns(j, carry):
-        layer, row = order(j)
-        i = layer * 4 + row
-        at = w_cols(i, core)
-        product = mm(n_t[...], gy[:, at])
-        from_partner(i).wait_recv()
-        both = (product + crx[i].astype(F32)).astype(BF16)
-
-        @pl.when(lax.rem(j, 4) < 3)
-        def _():
-            w[:, at] = both
-            to_owner(layer, row).start()
-
-        @pl.when(lax.rem(j, 4) == 3)
-        def _():
-            rs_rx[layer, y] = both
-        return carry
-
-    lax.fori_loop(0, N_CHIP, own_columns, 0)
-
     run[...] = jnp.zeros_like(run)
 
     def local_grads(i, carry):
@@ -422,13 +358,80 @@
 
     pair(1).start()
 
+    def w_cols(i, parity):
+        return pl.ds(pl.multiple_of((2 * i + parity) * COLS_W, COLS_W), COLS_W)
+
+    def to_partner(i):
+        return remote(w.at[:, w_cols(i, 1 - core)], crx.at[i], cs_s.at[i], cs_r.at[i], partner, h)
+
+    def from_partner(i):
+        return remote(w.at[:, w_cols(i, core)], crx.at[i], cs_s.at[i], cs_r.at[i], partner, h)
+
+    def order(j):
+        return jnp.where(j < 4, 1 - zl, zl), lax.rem(y + 1 + lax.rem(j, 4), 4)
+
+    def to_owner(layer, row):
+        return remote(w.at[:, w_cols(layer * 4 + row, core)], rs_rx.at[layer, y],
+                      ps_s.at[layer, row], ps_r.at[layer, y], zl * 8 + row * 2 + core, h)
+
+    def other_columns(j, carry):
+        layer, row = order(j)
+        i = layer * 4 + row
+        at = w_cols(i, 1 - core)
+        w[:, at] = mm(n_t[...], gy[:, at]).astype(BF16)
+        to_partner(i).start()
+        return carry
+
+    lax.fori_loop(0, N_CHIP, other_columns, 0)
+
+    chip_state(1)
+
+    own_w.wait()
+    for d in range(1, N_HEAD):
+        src = lax.rem(h + d, N_HEAD)
+        remote(w_piece(h), wcol.at[src, own_part], wa_s.at[d], wa_r.at[src], c, src).wait_recv()
+
+    def w_half(part, half):
+        return wcol.at[:, part, pl.ds(half * (W_ROWS // 2), W_ROWS // 2)]
+
+    def w_y(part, half, to):
+        return remote(w_half(part, half), w_half(part, half), wg_s.at[half], wg_r.at[half], to, h)
+
+    def w_core(part, i):
+        return remote(wcol.at[:, part], wcol.at[:, part], wg_s.at[2 + i], wg_r.at[2 + i], partner, h)
+
+    w_y(own_part, 0, y_down).start()
+    w_y(own_part, 1, y_up).start()
+    w_core(own_part, 0).start()
+
+    def own_columns(j, carry):
+        layer, row = order(j)
+        i = layer * 4 + row
+        at = w_cols(i, core)
+        product = mm(n_t[...], gy[:, at])
+        from_partner(i).wait_recv()
+        both = (product + crx[i].astype(F32)).astype(BF16)
+
+        @pl.when(lax.rem(j, 4) < 3)
+        def _():
+            w[:, at] = both
+            to_owner(layer, row).start()
+
+        @pl.when(lax.rem(j, 4) == 3)
+        def _():
+            rs_rx[layer, y] = both
+        return carry
+
+    lax.fori_loop(0, N_CHIP, own_columns, 0)
+
     arrive(west, 0)
     go(west, 0, 6, east)
     arrive(east, 1)
     go(east, 1, 7, west)
-
-    chip_state(1)
     chip_entry(1)
+    arrive(zp, 0)
+    go(zp, 0, 8, east)
+    go(zp, 0, 10, west)
     own_entry(1)
 
     def backward(b, carry):
@@ -450,10 +453,9 @@
 
     lax.fori_loop(0, NBLK, backward, 0)
 
-    for half in range(2):
-        arrive(zp, half)
-        go(zp, half, 8 + half, east)
-        go(zp, half, 10 + half, west)
+    arrive(zp, 1)
+    go(zp, 1, 9, east)
+    go(zp, 1, 11, west)
 
     w_y(far_part, 0, y_up).wait_recv()
     w_y(far_part, 1, y_down).wait_recv()
@@ -548,13 +550,9 @@
 
 
 def hand_over(*refs):
-    sems = refs[-1]
-    count = (len(refs) - 1) // 2
-    copies = [pltpu.make_async_copy(refs[i], refs[count + i], sems.at[i]) for i in range(count)]
-    for copy in copies:
-        copy.start()
-    for copy in copies:
-        copy.wait()
+    count = len(refs) // 2
+    for src, dst in zip(refs[:count], refs[count:]):
+        dst[...] = src[...]
 
 
 def per_device(q_in, k_in, v_in, log_decay, block_doc, w_out, grad_y):
@@ -623,12 +621,15 @@
             collective_id=0, has_side_effects=True, vmem_limit_bytes=63 << 20),
         name="attention_and_projection",
     )(block_doc, log_decay.T, q_in, k_in, v_in, w_out, grad_y)
+    steps = 4
+    specs = tuple(
+        pl.BlockSpec((one.shape[0] // steps, one.shape[1]), lambda i: (i, 0)) for one in shapes)
     return pl.pallas_call(
         hand_over,
         out_shape=shapes,
-        in_specs=[hbm] * 5,
-        out_specs=(hbm,) * 5,
-        scratch_shapes=[dma((5,))],
+        grid=(steps,),
+        in_specs=specs,
+        out_specs=specs,
         name="results",
     )(*results)
 

time: 265 us -> 117 us (0.44)
  the two profiles are of different devices: /device:TPU:0 before, /device:TPU:11 now
where the time goes in v3:
time: 117 us; the launch traced here: 116 us
  Pallas kernels  116 us (99%)
    pallas_call x1, Pallas kernels, per_device(): pl.pallas_call(kernel, out_shape=shapes, in_specs=[pl.BlockSpec(memory_sp...  111 us
    pallas_call x1, Pallas kernels, per_device(): pl.pallas_call(hand_over, out_shape=shapes, grid=(steps,), in_specs=specs...  4.58 us

profile of v3, /device:TPU:11, one launch (start us, length us, event | category | flops | bytes accessed | tf_op | source)
XLA Modules:
  0.0 116.4 jit_solution(14266580349283940539)
XLA Ops:
  0.6 111.2 %attention_and_projection.1 = (bf16[768,768]{1,0:T(8,128)(2,1)}, bf16[768,512]{1,0:T(8,128)(2,1)}, bf16[768,512]{1,0:T(8,128)(2,1)}, bf16[768,512]{1,0:T(8,128)(2,1)}, bf16[512,384]{1,0:T(8,128)(2,1)}) custom-call(s32[3]{0:T(128)} %docs.1, f32[4,768]{1,0:T(4,128)} %bitcast.1, bf16[768,512]{1,0:T(8,128)(2,1)} %q_hbm.1, bf16[768,512]{1,0:T(8,128)(2,1)} %k_hbm.1, ...), custom_call_target="tpu_custom_call" | custom-call | tf_op jit(solution)/shard_map/attention_and_projection/pallas_call | solution.py:569
  111.8 4.6 %results.1 = (bf16[768,768]{1,0:T(8,128)(2,1)}, bf16[768,512]{1,0:T(8,128)(2,1)}, bf16[768,512]{1,0:T(8,128)(2,1)}, bf16[768,512]{1,0:T(8,128)(2,1)}, bf16[512,384]{1,0:T(8,128)(2,1)}) custom-call(bf16[768,768]{1,0:T(8,128)(2,1)} %get-tuple-element.10.refs_0_, bf16[768,512]{1,0:T(8,128)(2,1)} %get-tuple-element.11.refs_1_, ...), custom_call_target="tpu_custom_call" | custom-call | tf_op jit(solution)/shard_map/results/pallas_call | solution.py:627

commit v4 on v3

--- a/solution.py
+++ b/solution.py
@@ -72,36 +72,55 @@
     loads = [
         pltpu.make_async_copy(src, dst, lsem.at[i])
         for i, (src, dst) in enumerate(
-            [(k_hbm, k), (v_hbm, v), (q_hbm, q), (w_hbm, w), (gy_hbm, gy)])
+            [(k_hbm, k), (v_hbm, v), (q_hbm, q)])
     ]
+    step_k = 1024
+    steps_k = D // step_k
+
+    def load_columns(i):
+        at = pl.ds(pl.multiple_of(i * step_k, step_k), step_k)
+        return [
+            pltpu.make_async_copy(w_hbm.at[:, at], w.at[:, at], lsem.at[4 + i]),
+            pltpu.make_async_copy(gy_hbm.at[:, at], gy.at[:, at], lsem.at[4 + steps_k + i]),
+        ]
+
 
     def w_piece(to):
         return w_hbm.at[pl.ds(pl.multiple_of(own_part * W_ROWS, W_ROWS), W_ROWS),
                         pl.ds(pl.multiple_of(to * COLS_Y, COLS_Y), COLS_Y)]
 
-    own_w = pltpu.make_async_copy(w_piece(h), wcol.at[h, own_part], lsem.at[5])
-    for copy in loads[:3]:
+    own_w = pltpu.make_async_copy(w_piece(h), wcol.at[h, own_part], lsem.at[3])
+    for copy in loads:
         copy.start()
 
+    def w_peer(d):
+        to_x, to_z = lax.rem(hx + d // 2, 4), lax.rem(hz + d % 2, 2)
+        return (z_peer if d % 2 else c), to_x * 2 + to_z
+
     barrier = pltpu.get_barrier_semaphore()
+    for d in range(1, N_HEAD, 2):
+        pl.semaphore_signal(barrier, inc=1, device_id=w_peer(d), device_id_type=MESH)
     for d in range(1, N_CTX):
         pl.semaphore_signal(barrier, inc=1, device_id=(lax.rem(c + d, N_CTX), h),
                             device_id_type=MESH)
     for d in range(1, N_HEAD):
         pl.semaphore_signal(barrier, inc=1, device_id=(c, lax.rem(h + d, N_HEAD)),
                             device_id_type=MESH)
-    pl.semaphore_wait(barrier, N_CTX + N_HEAD - 2)
+    pl.semaphore_wait(barrier, N_CTX + N_HEAD - 2 + N_HEAD // 2)
 
     def w_spread(d):
-        to = lax.rem(h + d, N_HEAD)
-        return remote(w_piece(to), wcol.at[h, own_part], wa_s.at[d], wa_r.at[h], c, to)
+        to_c, to = w_peer(d)
+        return remote(w_piece(to), wcol.at[h, own_part], wa_s.at[d], wa_r.at[h], to_c, to)
 
     def scal_spread(d):
         return remote(scal, scal_rx.at[c], sc_s.at[d], sc_r.at[c], lax.rem(c + d, N_CTX), h)
 
-    for copy in loads[3:]:
-        copy.start()
     own_w.start()
+    for d in range(1, N_HEAD):
+        w_spread(d).start()
+    for i in range(steps_k):
+        for copy in load_columns(i):
+            copy.start()
     at_row = lax.broadcasted_iota(jnp.int32, (BL, BL), 0)
     at_col = lax.broadcasted_iota(jnp.int32, (BL, BL), 1)
     lower = at_row >= at_col
@@ -272,15 +291,12 @@
 
     chip_state(0)
 
-    for d in range(1, N_HEAD):
-        w_spread(d).start()
-
-    loads[3].wait()
-    loads[4].wait()
+
     gn[...] = jnp.zeros_like(gn)
-    step_k = 1024
 
     def grad_normed(i, carry):
+        for copy in load_columns(i):
+            copy.wait()
         at = pl.ds(pl.multiple_of(i * step_k, step_k), step_k)
         gn[...] += mm(gy[:, at], w[:, at], NT)
         return carry
@@ -374,43 +390,20 @@
         return remote(w.at[:, w_cols(layer * 4 + row, core)], rs_rx.at[layer, y],
                       ps_s.at[layer, row], ps_r.at[layer, y], zl * 8 + row * 2 + core, h)
 
-    def other_columns(j, carry):
+    def columns(j, carry):
         layer, row = order(j)
         i = layer * 4 + row
-        at = w_cols(i, 1 - core)
+        at = pl.ds(pl.multiple_of(i * 2 * COLS_W, 2 * COLS_W), 2 * COLS_W)
         w[:, at] = mm(n_t[...], gy[:, at]).astype(BF16)
         to_partner(i).start()
         return carry
 
-    lax.fori_loop(0, N_CHIP, other_columns, 0)
-
-    chip_state(1)
-
-    own_w.wait()
-    for d in range(1, N_HEAD):
-        src = lax.rem(h + d, N_HEAD)
-        remote(w_piece(h), wcol.at[src, own_part], wa_s.at[d], wa_r.at[src], c, src).wait_recv()
-
-    def w_half(part, half):
-        return wcol.at[:, part, pl.ds(half * (W_ROWS // 2), W_ROWS // 2)]
-
-    def w_y(part, half, to):
-        return remote(w_half(part, half), w_half(part, half), wg_s.at[half], wg_r.at[half], to, h)
-
-    def w_core(part, i):
-        return remote(wcol.at[:, part], wcol.at[:, part], wg_s.at[2 + i], wg_r.at[2 + i], partner, h)
-
-    w_y(own_part, 0, y_down).start()
-    w_y(own_part, 1, y_up).start()
-    w_core(own_part, 0).start()
-
-    def own_columns(j, carry):
+    def chip_sum(j):
         layer, row = order(j)
         i = layer * 4 + row
         at = w_cols(i, core)
-        product = mm(n_t[...], gy[:, at])
         from_partner(i).wait_recv()
-        both = (product + crx[i].astype(F32)).astype(BF16)
+        both = (w[:, at].astype(F32) + crx[i].astype(F32)).astype(BF16)
 
         @pl.when(lax.rem(j, 4) < 3)
         def _():
@@ -420,9 +413,36 @@
         @pl.when(lax.rem(j, 4) == 3)
         def _():
             rs_rx[layer, y] = both
-        return carry
-
-    lax.fori_loop(0, N_CHIP, own_columns, 0)
+
+    def columns_and_sum(j, carry):
+        columns(j, carry)
+        chip_sum(j - 2)
+        return carry
+
+    lax.fori_loop(0, 2, columns, 0)
+    chip_state(1)
+
+    own_w.wait()
+    for d in range(1, N_HEAD):
+        from_c, src = w_peer(d)
+        remote(w_piece(h), wcol.at[src, own_part], wa_s.at[d], wa_r.at[src], from_c, src).wait_recv()
+
+    def w_half(part, half):
+        return wcol.at[:, part, pl.ds(half * (W_ROWS // 2), W_ROWS // 2)]
+
+    def w_y(part, half, to):
+        return remote(w_half(part, half), w_half(part, half), wg_s.at[half], wg_r.at[half], to, h)
+
+    def w_core(part, i):
+        return remote(wcol.at[:, part], wcol.at[:, part], wg_s.at[2 + i], wg_r.at[2 + i], partner, h)
+
+    w_y(own_part, 0, y_down).start()
+    w_y(own_part, 1, y_up).start()
+    w_core(own_part, 0).start()
+
+    lax.fori_loop(2, N_CHIP, columns_and_sum, 0)
+    chip_sum(jnp.int32(N_CHIP - 2))
+    chip_sum(jnp.int32(N_CHIP - 1))
 
     arrive(west, 0)
     go(west, 0, 6, east)
@@ -606,7 +626,7 @@
             pltpu.VMEM((2, 12, 8, DH), F32),
             pltpu.VMEM((HEADS, DH, DH), F32),
             pltpu.VMEM((TOK, COLS_Y), F32),
-            dma((6,)), dma((5,)),
+            dma((4 + 2 * (D // 1024),)), dma((5,)),
             dma((N_HEAD,)), dma((N_HEAD,)),
             dma((4,)), dma((4,)),
             dma((N_CTX,)), dma((N_CTX,)),

time: 117 us -> 103 us (0.88)
  the two profiles are of different devices: /device:TPU:11 before, /device:TPU:0 now
where the time goes in v4:
time: 103 us; the launch traced here: 101 us
  Pallas kernels  100 us (97%)
    pallas_call x1, Pallas kernels, per_device(): pl.pallas_call(kernel, out_shape=shapes, in_specs=[pl.BlockSpec(memory_sp...  95.9 us
    pallas_call x1, Pallas kernels, per_device(): pl.pallas_call(hand_over, out_shape=shapes, grid=(steps,), in_specs=specs...  4.58 us

profile of v4, /device:TPU:0, one launch (start us, length us, event | category | flops | bytes accessed | tf_op | source)
XLA Modules:
  0.0 101.1 jit_solution(7170861188340186666)
XLA Ops:
  0.6 95.9 %attention_and_projection.1 = (bf16[768,768]{1,0:T(8,128)(2,1)}, bf16[768,512]{1,0:T(8,128)(2,1)}, bf16[768,512]{1,0:T(8,128)(2,1)}, bf16[768,512]{1,0:T(8,128)(2,1)}, bf16[512,384]{1,0:T(8,128)(2,1)}) custom-call(s32[3]{0:T(128)} %docs.1, f32[4,768]{1,0:T(4,128)} %bitcast.1, bf16[768,512]{1,0:T(8,128)(2,1)} %q_hbm.1, bf16[768,512]{1,0:T(8,128)(2,1)} %k_hbm.1, ...), custom_call_target="tpu_custom_call" | custom-call | tf_op jit(solution)/shard_map/attention_and_projection/pallas_call | solution.py:589
  96.5 4.6 %results.1 = (bf16[768,768]{1,0:T(8,128)(2,1)}, bf16[768,512]{1,0:T(8,128)(2,1)}, bf16[768,512]{1,0:T(8,128)(2,1)}, bf16[768,512]{1,0:T(8,128)(2,1)}, bf16[512,384]{1,0:T(8,128)(2,1)}) custom-call(bf16[768,768]{1,0:T(8,128)(2,1)} %get-tuple-element.10.refs_0_, bf16[768,512]{1,0:T(8,128)(2,1)} %get-tuple-element.11.refs_1_, ...), custom_call_target="tpu_custom_call" | custom-call | tf_op jit(solution)/shard_map/results/pallas_call | solution.py:647

commit v5 on v4

--- a/solution.py
+++ b/solution.py
@@ -476,6 +476,9 @@
     arrive(zp, 1)
     go(zp, 1, 9, east)
     go(zp, 1, 11, west)
+    for half in range(2):
+        arrive(far, half)
+        go(far, half, 12 + half, zp)
 
     w_y(far_part, 0, y_up).wait_recv()
     w_y(far_part, 1, y_down).wait_recv()
@@ -504,9 +507,6 @@
     product(west, False)
     arrive(east, 0)
     product(east, False)
-    for half in range(2):
-        arrive(far, half)
-        go(far, half, 12 + half, zp)
     product(zp, False)
     product(far, False)
 
@@ -570,9 +570,18 @@
 
 
 def hand_over(*refs):
-    count = len(refs) // 2
-    for src, dst in zip(refs[:count], refs[count:]):
-        dst[...] = src[...]
+    *arrays, in_sem, out_sem = refs
+    count = len(arrays) // 3
+    srcs, dsts, bufs = arrays[:count], arrays[count:2 * count], arrays[2 * count:]
+    ins = [pltpu.make_async_copy(srcs[i], bufs[i], in_sem.at[i]) for i in range(count)]
+    outs = [pltpu.make_async_copy(bufs[i], dsts[i], out_sem.at[i]) for i in range(count)]
+    for copy in ins:
+        copy.start()
+    for i in range(count):
+        ins[i].wait()
+        outs[i].start()
+    for copy in outs:
+        copy.wait()
 
 
 def per_device(q_in, k_in, v_in, log_decay, block_doc, w_out, grad_y):
@@ -641,15 +650,12 @@
             collective_id=0, has_side_effects=True, vmem_limit_bytes=63 << 20),
         name="attention_and_projection",
     )(block_doc, log_decay.T, q_in, k_in, v_in, w_out, grad_y)
-    steps = 4
-    specs = tuple(
-        pl.BlockSpec((one.shape[0] // steps, one.shape[1]), lambda i: (i, 0)) for one in shapes)
     return pl.pallas_call(
         hand_over,
         out_shape=shapes,
-        grid=(steps,),
-        in_specs=specs,
-        out_specs=specs,
+        in_specs=[hbm] * 5,
+        out_specs=(hbm,) * 5,
+        scratch_shapes=[pltpu.VMEM(one.shape, BF16) for one in shapes] + [dma((5,)), dma((5,))],
         name="results",
     )(*results)
 

time: 103 us -> 99.2 us (0.963)
  the two profiles are of different devices: /device:TPU:0 before, /device:TPU:33 now
where the time goes in v5:
time: 99.2 us; the launch traced here: 99 us
  Pallas kernels  98.4 us (99%)
    pallas_call x1, Pallas kernels, per_device(): pl.pallas_call(kernel, out_shape=shapes, in_specs=[pl.BlockSpec(memory_sp...  95.1 us
    pallas_call x1, Pallas kernels, per_device(): pl.pallas_call(hand_over, out_shape=shapes, in_specs=[hbm] * 5, out_specs...  3.27 us

profile of v5, /device:TPU:33, one launch (start us, length us, event | category | flops | bytes accessed | tf_op | source)
XLA Modules:
  0.0 99.0 jit_solution(199505144271389067)
XLA Ops:
  0.6 95.1 %attention_and_projection.1 = (bf16[768,768]{1,0:T(8,128)(2,1)}, bf16[768,512]{1,0:T(8,128)(2,1)}, bf16[768,512]{1,0:T(8,128)(2,1)}, bf16[768,512]{1,0:T(8,128)(2,1)}, bf16[512,384]{1,0:T(8,128)(2,1)}) custom-call(s32[3]{0:T(128)} %docs.1, f32[4,768]{1,0:T(4,128)} %bitcast.1, bf16[768,512]{1,0:T(8,128)(2,1)} %q_hbm.1, bf16[768,512]{1,0:T(8,128)(2,1)} %k_hbm.1, ...), custom_call_target="tpu_custom_call" | custom-call | tf_op jit(solution)/shard_map/attention_and_projection/pallas_call | solution.py:598
  95.7 3.3 %results.1 = (bf16[768,768]{1,0:T(8,128)(2,1)}, bf16[768,512]{1,0:T(8,128)(2,1)}, bf16[768,512]{1,0:T(8,128)(2,1)}, bf16[768,512]{1,0:T(8,128)(2,1)}, bf16[512,384]{1,0:T(8,128)(2,1)}) custom-call(bf16[768,768]{1,0:T(8,128)(2,1)} %get-tuple-element.10.refs_0_, bf16[768,512]{1,0:T(8,128)(2,1)} %get-tuple-element.11.refs_1_, ...), custom_call_target="tpu_custom_call" | custom-call | tf_op jit(solution)/shard_map/results/pallas_call | solution.py:653
